TPU v7x, 256 devices: a whole 4x4x8 slice. The times are simulated.
256 devices in a mesh: ep: 64 (over z, y, core), kv: 4 (over x).
Axes of the slice: x: 4, y: 4, z: 8, core: 2. Of those that a mesh axis runs over, the one named last changes fastest.
Arguments:
- queries: bfloat16 [128, 2048], P('ep'), may hold values from -10 to 10
- key_pool: bfloat16 [1536, 128, 2048], P(('ep', 'kv')), may hold values from -4 to 4
- value_pool: bfloat16 [1536, 128, 2048], P(('ep', 'kv')), may hold values from -15 to 15
- page_table: int32 [128, 4, 3], P('ep', 'kv'), may hold values from 0 to 5, as said below
- lengths: int32 [128], P('ep'), may hold values from 2 to 1536, as said below
- prefill_attn: bfloat16 [8064, 2048], P('ep'), may hold values from -3 to 3
- residual: bfloat16 [8192, 2048], P('ep', 'kv'), may hold values from -64 to 64
- w_out: bfloat16 [2048, 2048], P(None, 'kv'), may hold values from -0.125 to 0.125
- norm_gain: float32 [2048], P('kv'), may hold values from 0.1 to 1.9
- router: bfloat16 [2048, 64], P('kv'), may hold values from -0.125 to 0.125
- w_gate: bfloat16 [64, 2048, 1024], P('ep', None, 'kv'), may hold values from -0.125 to 0.125
- w_up: bfloat16 [64, 2048, 1024], P('ep', None, 'kv'), may hold values from -0.125 to 0.125
- w_down: bfloat16 [64, 1024, 2048], P('ep', 'kv'), may hold values from -0.375 to 0.375
- final_gain: float32 [2048], P('kv'), may hold values from 0.1 to 1.9
- routes: int32 [8192, 8], P('ep'), may hold values from 0 to 63, all different within a row; in each aligned block of 128 rows (0 to 127, 128 to 255, ...) at most 32 rows name the same one
Outputs:
- output: bfloat16 [8192, 2048], P('ep', 'kv')
Inputs may be any that keep to these rules, and one draw needn't show every extreme that they name: `page_table`: the 2 x 3 entries of one group of requests at one holder are a permutation of 0 to 5. `lengths`: some request has length exactly 1536. `routes`: each row names 8 different experts; in the rows of one index of ep (aligned blocks of 128 rows) no expert is named more than 32 times, a bound that some block reaches.
All inputs are finite; a program needn't handle non-finite values.
Results may differ from a plain program's by a relative error of at most 0.009.
Values may be sent and summed in bfloat16 or wider, within the bound.
A program may use at most 128 MiB of HBM per device.

v0:
```python
import math

import jax
import jax.numpy as jnp
from jax import lax
from jax.sharding import PartitionSpec as P

D = 2048
HEADS = 16
HEAD_DIM = 128
TOP = 8


epsilon = 1e-06
floor_score = -1e30


def per_device(
    queries,
    key_pool,
    value_pool,
    page_table,
    lengths,
    prefill_attn,
    residual,
    w_out,
    norm_gain,
    router,
    w_gate,
    w_up,
    w_down,
    final_gain,
    routes,
):
    holders = lax.axis_size("kv")
    holder = lax.axis_index("kv")
    request_count = queries.shape[0]
    pool_pages = key_pool.shape[0]
    page_rows = key_pool.shape[1]
    pages_each = page_table.shape[2]
    query_heads = queries.reshape(request_count, HEADS, HEAD_DIM)
    page_slots = page_table[:, 0, :]
    picked_keys = key_pool.reshape(pool_pages, page_rows, HEADS, HEAD_DIM)[page_slots]
    picked_values = value_pool.reshape(pool_pages, page_rows, HEADS, HEAD_DIM)[page_slots]
    scores = jnp.einsum(
        "rhd,rjphd->rhjp", query_heads, picked_keys, preferred_element_type=jnp.float32
    ) / math.sqrt(HEAD_DIM)
    page_number = jnp.arange(pages_each, dtype=jnp.int32) * holders + holder
    position = page_number[:, None] * page_rows + jnp.arange(page_rows, dtype=jnp.int32)[None, :]
    visible = position[None, None, :, :] < lengths[:, None, None, None]
    masked = jnp.where(visible, scores, floor_score)
    local_peak = jnp.max(masked, axis=(2, 3))
    weights = jnp.where(visible, jnp.exp(masked - local_peak[:, :, None, None]), 0.0)
    local_mass = jnp.sum(weights, axis=(2, 3))
    local_sum = jnp.einsum(
        "rhjp,rjphd->rhd",
        weights,
        picked_values.astype(jnp.float32),
        precision=lax.Precision.HIGHEST,
    )
    peak_rows, masses, gathered_sums = (
        lax.all_gather(local_peak[None], "kv", axis=0, tiled=True),
        lax.all_gather(local_mass[None], "kv", axis=0, tiled=True),
        lax.all_gather(local_sum[None], "kv", axis=0, tiled=True),
    )
    all_peak = jnp.max(peak_rows, axis=0)
    factors = jnp.exp(peak_rows - all_peak[None])
    all_mass = jnp.sum(masses * factors, axis=0)
    all_sum = jnp.sum(gathered_sums * factors[..., None], axis=0)
    decode_attn = (all_sum / all_mass[..., None]).reshape(request_count, D).astype(jnp.bfloat16)
    attn_rows = jnp.concatenate([prefill_attn, decode_attn], axis=0)
    hidden_state = residual.astype(jnp.float32) + jnp.dot(
        attn_rows, w_out, preferred_element_type=jnp.float32
    )
    scaled = (hidden_state * norm_gain).astype(jnp.bfloat16)
    square_sum, logit_parts = lax.psum(
        (
            jnp.sum(hidden_state * hidden_state, axis=1),
            jnp.dot(scaled, router, preferred_element_type=jnp.float32),
        ),
        "kv",
    )
    inv_first = lax.rsqrt(square_sum / D + epsilon)
    logits = logit_parts * inv_first[:, None]
    normed = (hidden_state * norm_gain * inv_first[:, None]).astype(jnp.bfloat16)
    row_count = residual.shape[0]
    expert_count = router.shape[1]
    capacity = min(row_count, 2 * row_count * TOP // expert_count)
    matches = routes[:, :, None] == jnp.arange(expert_count, dtype=jnp.int32)[None, None, :]
    chosen = jnp.sum(jnp.where(matches, logits[:, None, :], 0.0), axis=2)
    raised = jnp.exp(chosen)
    gate_weights = raised / jnp.sum(raised, axis=1, keepdims=True)
    one_hot = matches.reshape(row_count * TOP, expert_count).astype(jnp.int32)
    earlier = jnp.cumsum(one_hot, axis=0) - one_hot
    slot_index = jnp.sum(earlier * one_hot, axis=1)
    target = routes.reshape(-1) * capacity + slot_index
    source_row = jnp.arange(row_count * TOP, dtype=jnp.int32) // TOP
    filler = jnp.zeros((expert_count * capacity,), jnp.int32).at[target].set(source_row)
    present = jnp.zeros((expert_count * capacity,), jnp.bool_).at[target].set(True)
    gate_local = w_gate[0]
    up_local = w_up[0]
    down_local = w_down[0]
    full_rows = lax.all_gather(normed, "kv", axis=1, tiled=True)
    picked = full_rows[filler]
    arrived = lax.all_to_all(
        jnp.where(present[:, None], picked, jnp.zeros_like(picked)).reshape(
            expert_count, capacity, full_rows.shape[1]
        ),
        "ep",
        split_axis=0,
        concat_axis=0,
        tiled=True,
    )
    inbound = arrived.reshape(-1, arrived.shape[2])
    gate_proj = jnp.dot(inbound, gate_local, preferred_element_type=jnp.float32)
    up_proj = jnp.dot(inbound, up_local, preferred_element_type=jnp.float32)
    activation = (jax.nn.silu(gate_proj) * up_proj).astype(jnp.bfloat16)
    feature_cols = residual.shape[1]
    summed = lax.psum_scatter(
        lax.dot_general(
            down_local, activation, (((0,), (1,)), ((), ())), preferred_element_type=jnp.float32
        ).astype(jnp.bfloat16),
        "kv",
        scatter_dimension=0,
        tiled=True,
    ).astype(jnp.float32)
    expert_out = summed.T.astype(jnp.bfloat16).reshape(
        arrived.shape[0], arrived.shape[1], feature_cols
    )
    returned = lax.all_to_all(expert_out, "ep", split_axis=0, concat_axis=0, tiled=True)
    back_rows = (
        returned.reshape(-1, feature_cols)[target]
        .reshape(row_count, TOP, feature_cols)
        .astype(jnp.float32)
    )
    combined = hidden_state + jnp.sum(back_rows * gate_weights[:, :, None], axis=1)
    square_two = lax.psum(jnp.sum(combined * combined, axis=1), "kv")
    return (combined * lax.rsqrt(square_two / D + epsilon)[:, None] * final_gain).astype(
        jnp.bfloat16
    )


def solution(mesh):
    placed = (
        P("ep", None),
        P(("ep", "kv"), None, None),
        P(("ep", "kv"), None, None),
        P("ep", "kv", None),
        P("ep"),
        P("ep", None),
        P("ep", "kv"),
        P(None, "kv"),
        P("kv"),
        P("kv", None),
        P("ep", None, "kv"),
        P("ep", None, "kv"),
        P("ep", "kv", None),
        P("kv"),
        P("ep", None),
    )
    return jax.shard_map(
        per_device, mesh=mesh, in_specs=placed, out_specs=P("ep", "kv"), check_vma=False
    )
```

profile of v0, /device:TPU:24, one launch (start us, length us, event | category | flops | bytes accessed | tf_op | source)
XLA Modules:
  0.0 522.8 jit_solution(8753484082852939923)
XLA Ops:
  6.5 0.8 broadcast_multiply_fusion.1
  7.4 0.8 copy.33
  8.2 0.1 eq.36
  8.3 0.1 eq.32
  8.4 4.6 copy.45
  13.0 0.1 reshape.180
  13.1 4.6 copy.44
  17.7 4.6 gather_fusion.1
  22.3 4.6 gather_fusion
  27.1 3.3 fusion.2
  30.4 0.1 fusion.25
  30.5 0.2 fusion.23
  30.7 2.1 fusion
  32.8 12.2 %all-gather = f32[8,16,128]{2,1,0:T(8,128)S(1)} all-gather(f32[2,16,128]{2,1,0:T(8,128)S(1)} %bitcast.96), channel_id=2, replica_groups=mesh['ep'=64,'kv'=4] {'kv'}, dimensions={0}, use_global_device_ids=true | all-gather | bytes 81920 | tf_op jit(solution)/shard_map/all_gather | solution.py:64
  45.1 9.4 %all-gather.4 = f32[4,2,16]{2,1,0:T(2,128)S(1)} all-gather(f32[1,2,16]{2,1,0:T(2,128)S(1)} %bitcast.102), channel_id=4, replica_groups=mesh['ep'=64,'kv'=4] {'kv'}, dimensions={0}, use_global_device_ids=true | all-gather | bytes 640 | tf_op jit(solution)/shard_map/all_gather | solution.py:63
  54.4 7.0 %all-gather.3 = f32[4,2,16]{2,1,0:T(2,128)S(1)} all-gather(f32[1,2,16]{2,1,0:T(2,128)S(1)} %bitcast.100), channel_id=3, replica_groups=mesh['ep'=64,'kv'=4] {'kv'}, dimensions={0}, use_global_device_ids=true | all-gather | bytes 640 | tf_op jit(solution)/shard_map/all_gather | solution.py:62
  61.4 0.1 multiply_reduce_fusion.2
  61.5 0.1 fusion.27
  61.6 0.5 multiply_reduce_fusion.1
  62.2 0.2 fusion.19
  62.3 16.7 %all-reduce = (f32[128]{0:T(128)S(1)}, f32[128,64]{0,1:T(8,128)S(1)}) all-reduce(f32[128]{0:T(128)S(1)} %get-tuple-element.13, f32[128,64]{0,1:T(8,128)S(1)} %fusion.19), channel_id=1, replica_groups=mesh['ep'=64,'kv'=4] {'kv'}, use_global_device_ids=true, to_apply=%region_10.11 | all-reduce | flops 8320 | bytes 66560 | tf_op jit(solution)/shard_map/psum | solution.py:76
  79.1 0.1 multiply_convert_fusion.1
  79.2 12.8 %all_gather.15 = bf16[128,2048]{1,0:T(8,128)(2,1)S(1)} all-gather(bf16[128,512]{1,0:T(8,128)(2,1)S(1)} %multiply_convert_fusion.1), channel_id=1, replica_groups=mesh['ep'=64,'kv'=4] {'kv'}, dimensions={1}, use_global_device_ids=true | all-gather | bytes 655360 | tf_op jit(solution)/shard_map/all_gather | solution.py:103
  92.0 0.1 copy.32
  92.1 0.1 mul.117
  92.2 18.0 %reduce-window.6 = s32[64,8,128]{2,1,0:T(8,128)S(1)} reduce-window(s32[64,8,128]{2,1,0:T(8,128)S(1)} %fusion.18, s32[]{:T(128)} %constant.24.clone.1), window={size=1x1x128 pad=0_0x0_0x127_0}, to_apply=%region_5.6 | reduce-window | flops 8323072 | bytes 524292 | tf_op jit(solution)/shard_map/reduce-window
  110.2 0.1 slice.16
  110.3 0.1 copy.35
  110.5 0.1 copy.36
  110.6 0.1 broadcast_add_fusion
  110.8 4.5 scatter_custom_fusion.1
  115.4 4.3 scatter_custom_fusion
  119.7 0.1 broadcast_in_dim.94
  119.8 11.0 %gather_fusion.2 = bf16[2048,2048]{1,0:T(8,128)(2,1)} fusion(bf16[128,2048]{1,0:T(8,128)(2,1)S(1)} %all_gather.15, s32[2048]{0:T(1024)S(1)} %fusion.26), kind=kCustom, calls=%fused_computation.2 | custom fusion | bytes 16785408 | tf_op jit(solution)/shard_map/gather | solution.py:104
  130.8 7.2 %broadcast_select_fusion = bf16[64,32,2048]{2,1,0:T(8,128)(2,1)} fusion(bf16[64,32,2048]{2,1,0:T(8,128)(2,1)} %bitcast.82, pred[64,32]{1,0:T(8,128)(4,1)S(1)} %broadcast_in_dim.94), kind=kLoop, calls=%fused_computation.7 | loop fusion | flops 4194304 | bytes 16779264 | tf_op jit(solution)/shard_map/jit(_where)/select_n | solution.py:106
  138.1 198.1 %all_to_all.10 = bf16[64,32,2048]{2,1,0:T(8,128)(2,1)S(1)} all-to-all(bf16[64,32,2048]{2,1,0:T(8,128)(2,1)} %broadcast_select_fusion), channel_id=1, replica_groups=mesh['ep'=64,'kv'=4] {'ep'}, dimensions={0} | all-to-all | bytes 16777216 | tf_op jit(solution)/shard_map/all_to_all | solution.py:105
  336.2 3.2 copy-done.2
  339.4 3.8 fusion.9
  343.2 16.8 %convert_bitcast_fusion = bf16[2048,2048]{0,1:T(8,128)(2,1)} fusion(bf16[2048,2048]{1,0:T(8,128)(2,1)} %bitcast.86, f32[2048,256]{1,0:T(8,128)} %fusion.9, bf16[1,256,2048]{2,1,0:T(8,128)(2,1)S(1)} %copy-done.12, bf16[1,2048,256]{2,1,0:T(8,128)(2,1)} %param.26), kind=kOutput, calls=%fused_computation.6 | convolution fusion | flops 4302307328 | bytes 20971520 | tf_op jit(solution)/shard_map/dot_general | solution.py:120
  360.1 77.8 %reduce-scatter.2.cloned.1.call-done = bf16[512,2048]{0,1:T(8,128)(2,1)} async-done(((bf16[2048,2048]{0,1:T(8,128)(2,1)}), bf16[512,2048]{0,1:T(8,128)(2,1)}) %reduce-scatter.2.cloned.1.call-update) | async-done | bytes 2097168 | tf_op jit(solution)/shard_map/reduce_scatter | solution.py:119
  437.9 10.7 %all-to-all-start.1 = ((bf16[64,32,512]{2,1,0:T(8,128)(2,1)}), bf16[64,32,512]{2,1,0:T(8,128)(2,1)}, u32[]{:S(2)}, u32[]{:S(2)}) async-start(bf16[64,32,512]{2,1,0:T(8,128)(2,1)} %bitcast.91), calls=%async_computation.2 | async-start | bytes 4194304 | tf_op jit(solution)/shard_map/all_to_all | solution.py:130
  448.7 0.1 copy.37
  448.8 51.0 %all-to-all-done.1 = bf16[64,32,512]{2,1,0:T(8,128)(2,1)} async-done(((bf16[64,32,512]{2,1,0:T(8,128)(2,1)}), bf16[64,32,512]{2,1,0:T(8,128)(2,1)}, u32[]{:S(2)}, u32[]{:S(2)}) %all-to-all-start.1) | async-done | bytes 2097184 | tf_op jit(solution)/shard_map/all_to_all | solution.py:130
  499.8 6.0 %gather_fusion.3 = bf16[1024,512]{1,0:T(8,128)(2,1)S(1)} fusion(bf16[2048,512]{1,0:T(8,128)(2,1)} %bitcast.22, s32[1024]{0:T(1024)S(1)} %broadcast_clamp_fusion), kind=kCustom, calls=%fused_computation.3 | custom fusion | bytes 2101248 | tf_op jit(solution)/shard_map/gather | solution.py:132
  505.8 0.7 fusion.5
  506.5 0.1 multiply_reduce_fusion
  506.6 8.6 %psum.23 = f32[128]{0:T(128)S(1)} all-reduce(f32[128]{0:T(128)S(1)} %get-tuple-element.7), channel_id=1, replica_groups=mesh['ep'=64,'kv'=4] {'kv'}, use_global_device_ids=true, to_apply=%region_18.19 | all-reduce | flops 128 | bytes 1024 | tf_op jit(solution)/shard_map/psum | solution.py:137
  515.2 0.8 multiply_convert_fusion
  (55 shorter events, 0.5 us)
Async XLA Ops:
  6.5 55.1 %copy-start = (bf16[2048,512]{1,0:T(8,128)(2,1)S(1)}, bf16[2048,512]{1,0:T(8,128)(2,1)}, u32[]{:S(2)}) copy-start(bf16[2048,512]{1,0:T(8,128)(2,1)} %param.22) | copy-start | bytes 6291460
  6.5 431.4 %reduce-scatter.2.cloned.1.call-start = ((), (), s32[]{:S(2)}) async-start(), calls=%async_computation.3 | async-start | bytes 10485760 | tf_op jit(solution)/shard_map/reduce_scatter | solution.py:119
  8.4 4.6 copy-start.9
  8.4 4.7 copy-start.7
  27.0 3.3 copy-start.10
  27.0 3.7 copy-start.3
  27.1 34.5 %copy-start.13 = (bf16[126,2048]{1,0:T(8,128)(2,1)S(1)}, bf16[126,2048]{1,0:T(8,128)(2,1)}, u32[]{:S(2)}) copy-start(bf16[126,2048]{1,0:T(8,128)(2,1)} %param.20) | copy-start | bytes 1548292
  27.1 34.5 %copy-start.14 = (bf16[128,512]{1,0:T(8,128)(2,1)S(1)}, bf16[128,512]{1,0:T(8,128)(2,1)}, u32[]{:S(2)}) copy-start(bf16[128,512]{1,0:T(8,128)(2,1)} %param.21) | copy-start | bytes 393220
  30.7 31.5 %copy-start.4 = (bf16[512,64]{0,1:T(8,128)(2,1)S(1)}, bf16[512,64]{0,1:T(8,128)(2,1)}, u32[]{:S(2)}) copy-start(bf16[512,64]{0,1:T(8,128)(2,1)} %param.24) | copy-start | bytes 196612
  30.7 31.5 %copy-start.6 = (f32[512]{0:T(512)S(1)}, f32[512]{0:T(512)}, u32[]{:S(2)}) copy-start(f32[512]{0:T(512)} %param.23) | copy-start | bytes 6148
  138.1 201.3 %copy-start.11 = (bf16[1,2048,256]{2,1,0:T(8,128)(2,1)S(1)}, bf16[1,2048,256]{2,1,0:T(8,128)(2,1)}, u32[]{:S(2)}) copy-start(bf16[1,2048,256]{2,1,0:T(8,128)(2,1)} %param.25) | copy-start | bytes 3145732
  336.2 3.2 copy-start.2
  339.4 3.8 copy-start.12
  360.0 88.6 %copy-start.5 = (s32[128,8]{0,1:T(8,128)S(1)}, s32[128,8]{0,1:T(8,128)}, u32[]{:S(2)}) copy-start(s32[128,8]{0,1:T(8,128)} %param.29) | copy-start | bytes 12292
  437.9 61.9 %all-to-all-start.1 = ((bf16[64,32,512]{2,1,0:T(8,128)(2,1)}), bf16[64,32,512]{2,1,0:T(8,128)(2,1)}, u32[]{:S(2)}, u32[]{:S(2)}) async-start(bf16[64,32,512]{2,1,0:T(8,128)(2,1)} %bitcast.91), calls=%async_computation.2 | async-start | bytes 4194304 | tf_op jit(solution)/shard_map/all_to_all | solution.py:130
  499.8 15.4 %copy-start.8 = (f32[512]{0:T(512)S(1)}, f32[512]{0:T(512)}, u32[]{:S(2)}) copy-start(f32[512]{0:T(512)} %param.28) | copy-start | bytes 6148
  499.8 16.2 %copy-start.1 = (bf16[2048,512]{1,0:T(8,128)(2,1)S(1)}, bf16[2048,512]{1,0:T(8,128)(2,1)}, u32[]{:S(2)}) copy-start(bf16[2048,512]{1,0:T(8,128)(2,1)} %param.22) | copy-start | bytes 6291460
Sparse Core Ops, SparseCore 0:
  360.2 77.6 reduce-scatter.1
where the time goes:
time: 524 us; the launch traced here: 523 us
  blocking collectives  265 us (51%)
  waiting for transfers between devices  129 us (25%)
  local copies, waits for them, and re-layouts  49.4 us (9%)
  other arithmetic  28.7 us (5%)
  matrix products  26.7 us (5%)
  between operations  13.7 us (3%)
  starting transfers between devices  10.7 us (2%)
    all_to_all x1, blocking collectives, per_device(): lax.all_to_all(jnp.where(present[:, None], picked, jnp.zeros_like(picked)...  198 us
    reduce_scatter x1, waiting for transfers between devices, per_device(): lax.psum_scatter(lax.dot_general(down_local, activation, (((0,), (1,)), (...  77.8 us
    all_to_all x1, waiting for transfers between devices, per_device(): lax.all_to_all(expert_out, 'ep', split_axis=0, concat_axis=0, tiled=True)  51 us
    another operation x3, other arithmetic  18.2 us
    dot_general x1, matrix products, per_device(): lax.dot_general(down_local, activation, (((0,), (1,)), ((), ())), preferr...  16.8 us
    psum x1, blocking collectives, per_device(): lax.psum((jnp.sum(hidden_state * hidden_state, axis=1), jnp.dot(scaled, r...  16.7 us
    unnamed x34, local copies, waits for them, and re-layouts  13.3 us
    all_gather x1, blocking collectives, per_device(): full_rows = lax.all_gather(normed, 'kv', axis=1, tiled=True)  12.8 us
  transfers between devices with their start and end apart: 2, of which 2 were waited for; matrix products, arithmetic and copies ran while one was open for 0% of the time, Pallas kernels for 0%

commit v1 on v0

v1 whole, which is shorter than its diff:
```python
import math

import jax
import jax.numpy as jnp
from jax import lax
from jax.sharding import PartitionSpec as P

D = 2048
HEADS = 16
HEAD_DIM = 128
TOP = 8


epsilon = 1e-06
floor_score = -1e30


def split_two(v):
    high = v.astype(jnp.bfloat16)
    low = (v - high.astype(jnp.float32)).astype(jnp.bfloat16)
    return high, low


def per_device(
    queries,
    key_pool,
    value_pool,
    page_table,
    lengths,
    prefill_attn,
    residual,
    w_out,
    norm_gain,
    router,
    w_gate,
    w_up,
    w_down,
    final_gain,
    routes,
):
    holders = lax.axis_size("kv")
    holder = lax.axis_index("kv")
    request_count = queries.shape[0]
    pool_pages, page_rows = key_pool.shape[0], key_pool.shape[1]
    pages_each = page_table.shape[2]
    row_count = residual.shape[0]
    feature_cols = residual.shape[1]
    expert_count = router.shape[1]
    share = min(row_count, 2 * row_count * TOP // expert_count) // holders

    gate_all = lax.all_gather(w_gate[0], "kv", axis=0)
    up_all = lax.all_gather(w_up[0], "kv", axis=0)
    down_all = lax.all_gather(w_down[0], "kv", axis=0)

    tokens = pool_pages * page_rows
    keys = key_pool.reshape(tokens, D)
    values = value_pool.reshape(tokens, D)
    head_of = jnp.arange(D, dtype=jnp.int32) // HEAD_DIM
    on_head = (head_of[None, :] == jnp.arange(HEADS, dtype=jnp.int32)[:, None])
    spread = jnp.where(on_head[None], queries[:, None, :], 0).reshape(request_count * HEADS, D)
    scores = lax.dot_general(
        spread, keys, (((1,), (1,)), ((), ())), preferred_element_type=jnp.float32
    ).reshape(request_count, HEADS, pool_pages, page_rows) / math.sqrt(HEAD_DIM)
    slots = page_table[:, 0, :]
    is_page = slots[:, :, None] == jnp.arange(pool_pages, dtype=jnp.int32)[None, None, :]
    page_number = jnp.arange(pages_each, dtype=jnp.int32) * holders + holder
    start = jnp.sum(jnp.where(is_page, page_number[None, :, None] * page_rows, 0), axis=1)
    owned = jnp.any(is_page, axis=1)
    position = start[:, :, None] + jnp.arange(page_rows, dtype=jnp.int32)[None, None, :]
    visible = (owned[:, :, None] & (position < lengths[:, None, None]))[:, None]
    masked = jnp.where(visible, scores, floor_score)
    local_peak = jnp.max(masked, axis=(2, 3))
    weights = jnp.where(visible, jnp.exp(masked - local_peak[:, :, None, None]), 0.0)
    local_mass = jnp.sum(weights, axis=(2, 3))
    high, low = split_two(weights.reshape(request_count * HEADS, tokens))
    wide = jnp.dot(
        jnp.concatenate([high, low], axis=0), values, preferred_element_type=jnp.float32
    ).reshape(2, request_count, HEADS, D)
    local_sum = jnp.sum(jnp.where(on_head[None], wide[0] + wide[1], 0.0), axis=1)
    pack = jnp.concatenate(
        [local_sum, jnp.repeat(local_peak, HEAD_DIM, axis=1), jnp.repeat(local_mass, HEAD_DIM, axis=1)],
        axis=0,
    )
    packs = lax.all_gather(pack, "kv", axis=0).reshape(holders, 3, request_count, D)
    peaks, masses = packs[:, 1], packs[:, 2]
    factors = jnp.exp(peaks - jnp.max(peaks, axis=0)[None])
    decode_attn = (
        jnp.sum(packs[:, 0] * factors, axis=0) / jnp.sum(masses * factors, axis=0)
    ).astype(jnp.bfloat16)
    attn_rows = jnp.concatenate([prefill_attn, decode_attn], axis=0)
    hidden_state = residual.astype(jnp.float32) + jnp.dot(
        attn_rows, w_out, preferred_element_type=jnp.float32
    )
    scaled = (hidden_state * norm_gain).astype(jnp.bfloat16)
    stats = jnp.concatenate(
        [
            jnp.dot(scaled, router, preferred_element_type=jnp.float32),
            jnp.sum(hidden_state * hidden_state, axis=1, keepdims=True),
            jnp.zeros((row_count, 63), jnp.float32),
        ],
        axis=1,
    )
    stats = jnp.sum(lax.all_gather(stats, "kv", axis=0), axis=0)
    inv_first = lax.rsqrt(stats[:, expert_count : expert_count + 1] / D + epsilon)
    logits = stats[:, :expert_count] * inv_first
    normed = (hidden_state * norm_gain * inv_first).astype(jnp.bfloat16)
    full_rows = lax.all_gather(normed, "kv", axis=1, tiled=True)

    experts = jnp.arange(expert_count, dtype=jnp.int32)
    named = jnp.any(routes[:, :, None] == experts[None, None, :], axis=1)
    raised = jnp.where(named, jnp.exp(logits), 0.0)
    gate_weights = raised / jnp.sum(raised, axis=1, keepdims=True)
    before = jnp.tril(jnp.ones((row_count, row_count), jnp.bfloat16), -1)
    rank = jnp.dot(before, named.astype(jnp.bfloat16), preferred_element_type=jnp.float32)
    code = jnp.where(named, rank, -1.0).astype(jnp.int32)
    mine = holder * share + jnp.arange(share, dtype=jnp.int32)
    at_slot = code[:, :, None] == mine[None, None, :]
    pick = at_slot.astype(jnp.bfloat16).reshape(row_count, expert_count * share)
    outbound = lax.dot_general(
        pick, full_rows, (((0,), (0,)), ((), ())), preferred_element_type=jnp.bfloat16
    ).reshape(expert_count, share, D)
    arrived = lax.all_to_all(outbound, "ep", split_axis=0, concat_axis=0, tiled=True)
    inbound = arrived.reshape(-1, D)
    total = jnp.zeros(inbound.shape, jnp.float32)
    for part in range(gate_all.shape[0]):
        gate_proj = jnp.dot(inbound, gate_all[part], preferred_element_type=jnp.float32)
        up_proj = jnp.dot(inbound, up_all[part], preferred_element_type=jnp.float32)
        activation = (jax.nn.silu(gate_proj) * up_proj).astype(jnp.bfloat16)
        total += jnp.dot(activation, down_all[part], preferred_element_type=jnp.float32)
    expert_out = total.astype(jnp.bfloat16).reshape(arrived.shape)
    returned = lax.all_to_all(expert_out, "ep", split_axis=0, concat_axis=0, tiled=True)
    mix = jnp.where(at_slot, gate_weights[:, :, None], 0.0).reshape(row_count, -1)
    high, low = split_two(mix)
    back = returned.reshape(-1, D)
    mixture = jnp.dot(high, back, preferred_element_type=jnp.float32) + jnp.dot(
        low, back, preferred_element_type=jnp.float32
    )
    parts = mixture.astype(jnp.bfloat16).reshape(row_count, holders, feature_cols)
    parts = lax.all_to_all(parts.transpose(1, 0, 2), "kv", split_axis=0, concat_axis=0, tiled=True)
    combined = hidden_state + jnp.sum(parts.astype(jnp.float32), axis=0)
    square_two = lax.psum(jnp.sum(combined * combined, axis=1), "kv")
    return (combined * lax.rsqrt(square_two / D + epsilon)[:, None] * final_gain).astype(
        jnp.bfloat16
    )


def solution(mesh):
    placed = (
        P("ep", None),
        P(("ep", "kv"), None, None),
        P(("ep", "kv"), None, None),
        P("ep", "kv", None),
        P("ep"),
        P("ep", None),
        P("ep", "kv"),
        P(None, "kv"),
        P("kv"),
        P("kv", None),
        P("ep", None, "kv"),
        P("ep", None, "kv"),
        P("ep", "kv", None),
        P("kv"),
        P("ep", None),
    )
    return jax.shard_map(
        per_device, mesh=mesh, in_specs=placed, out_specs=P("ep", "kv"), check_vma=False
    )
```

time: 524 us -> 301 us (0.57)
  blocking collectives: 265 us -> 125 us
  local copies, waits for them, and re-layouts: 49.4 us -> 2.47 us
  waiting for transfers between devices: 129 us -> 91.9 us
  matrix products: 26.7 us -> 50.1 us
  other arithmetic: 28.7 us -> 5.8 us
    all_to_all x1 -> x2, blocking collectives: 198 us -> 74.3 us  [the longest x1 63.1 us: per_device(): lax.all_to_all(outbound, 'ep', split_axis=0, concat_axis=0, tiled=True)]
    reduce_scatter x1 -> x0, waiting for transfers between devices: 77.8 us -> none  [per_device(): lax.psum_scatter(lax.dot_general(down_local, activation, (((0,), (1,)), (...]
    all_gather x0 -> x3, waiting for transfers between devices: none -> 39.3 us  [the longest x1 39.3 us: per_device(): down_all = lax.all_gather(w_down[0], 'kv', axis=0)]
    gather x4 -> x0, local copies, waits for them, and re-layouts: 26.2 us -> none  [the longest x1 11 us: per_device(): picked = full_rows[filler]]
    dot_general x4 -> x14, matrix products: 26 us -> 48.5 us  [the longest x4 29.4 us: per_device(): jnp.dot(activation, down_all[part], preferred_element_type=jnp.float32)]
    another operation x3 -> x0, other arithmetic: 18.2 us -> none
    psum x1 -> x0, blocking collectives: 16.7 us -> none  [per_device(): lax.psum((jnp.sum(hidden_state * hidden_state, axis=1), jnp.dot(scaled, r...]
    unnamed x34 -> x33, local copies, waits for them, and re-layouts: 13.3 us -> 0.23 us
  transfers between devices with their start and end apart: 2 -> 4, of which waited for: 2 -> 2; matrix products, arithmetic and copies ran while one was open for 0% -> 7% of each run, Pallas kernels for 0% -> 0%
where the time goes in v1:
time: 301 us; the launch traced here: 300 us
  blocking collectives  125 us (42%)
  waiting for transfers between devices  91.9 us (31%)
  matrix products  50.1 us (17%)
  between operations  13.4 us (4%)
  starting transfers between devices  10.9 us (4%)
  other arithmetic  5.8 us (2%)
    all_to_all x1, blocking collectives, per_device(): lax.all_to_all(outbound, 'ep', split_axis=0, concat_axis=0, tiled=True)  63.1 us
    all_to_all x1, waiting for transfers between devices, per_device(): lax.all_to_all(expert_out, 'ep', split_axis=0, concat_axis=0, tiled=True)  50.5 us
    all_gather x1, waiting for transfers between devices, per_device(): down_all = lax.all_gather(w_down[0], 'kv', axis=0)  39.3 us
    dot_general x4, matrix products, per_device(): jnp.dot(activation, down_all[part], preferred_element_type=jnp.float32)  29.4 us
    all_gather x1, blocking collectives, per_device(): full_rows = lax.all_gather(normed, 'kv', axis=1, tiled=True)  15.4 us
    all_gather x1, blocking collectives, per_device(): stats = jnp.sum(lax.all_gather(stats, 'kv', axis=0), axis=0)  14.3 us
    all_gather x1, blocking collectives, per_device(): lax.all_gather(pack, 'kv', axis=0).reshape(holders, 3, request_count, D)  12.6 us
    all_to_all x1, blocking collectives, per_device(): lax.all_to_all(parts.transpose(1, 0, 2), 'kv', split_axis=0, concat_axis=...  11.3 us
  transfers between devices with their start and end apart: 4, of which 2 were waited for; matrix products, arithmetic and copies ran while one was open for 7% of the time, Pallas kernels for 0%

profile of v1, /device:TPU:24, one launch (start us, length us, event | category | flops | bytes accessed | tf_op | source)
XLA Modules:
  0.0 300.1 jit_solution(8328937793961176170)
XLA Ops:
  6.6 0.7 all-gather.7.cloned.1.call-update
  7.3 0.7 all-gather.9.cloned.1.call-update
  8.1 0.7 all-gather.11.cloned.1.call-update
  8.8 0.5 iota_add_fusion.1
  9.3 0.1 copy.29
  9.4 0.1 fusion.137
  9.5 0.1 select_reduce_fusion.1
  9.6 0.1 fusion.135
  9.7 3.0 %fusion.153 = (f32[2,16]{1,0:T(2,128)S(1)}, f32[2,16,6,128]{3,1,2,0:T(8,128)S(1)}) fusion(bf16[6,128,2048]{2,1,0:T(8,128)(2,1)} %param.16, pred[16,2048]{1,0:T(8,128)(4,1)S(1)} %iota_compare_fusion.1, bf16[2,2048]{1,0:T(2,128)(2,1)S(1)} %copy-done.3, pred[2,6,128]{2,1,0:T(8,128)(4,1)S(1)} %fusion.135), kind=kOutput, calls=%fused_computation.181 | convolution fusion | flops 100802528 | bytes 3286656 | tf_op jit(solution)/shard_map/dot_general | solution.py:61
  12.7 0.1 broadcast_bitcast_fusion.1
  12.8 0.2 fusion.152
  13.1 0.1 eq.93
  13.3 0.1 broadcast_bitcast_fusion
  13.3 0.7 fusion.113
  14.0 0.1 select_reduce_fusion
  14.2 12.6 %all-gather.2 = f32[4,6,2048]{2,1,0:T(8,128)S(1)} all-gather(f32[1,6,2048]{2,1,0:T(8,128)S(1)} %maximum_bitcast_fusion), channel_id=2, replica_groups=mesh['ep'=64,'kv'=4] {'kv'}, dimensions={0}, use_global_device_ids=true | all-gather | bytes 245760 | tf_op jit(solution)/shard_map/all_gather | solution.py:84
  26.8 0.1 copy.32
  26.9 0.1 fusion.118
  27.1 0.1 pad.2.clone
  27.2 1.4 multiply_reduce_fusion.1
  28.6 0.2 fusion.97
  28.8 0.1 maximum_maximum_fusion
  28.9 14.3 %all-gather.1 = f32[512,128]{0,1:T(8,128)} all-gather(f32[128,128]{0,1:T(8,128)S(1)} %maximum_maximum_fusion), channel_id=3, replica_groups=mesh['ep'=64,'kv'=4] {'kv'}, dimensions={0}, use_global_device_ids=true | all-gather | bytes 327680 | tf_op jit(solution)/shard_map/all_gather | solution.py:103
  43.2 1.7 reshape.132
  44.9 1.1 reduce_sum.96
  46.1 0.1 multiply_convert_fusion.1
  46.2 15.4 %all_gather.28 = bf16[128,2048]{1,0:T(8,128)(2,1)S(1)} all-gather(bf16[128,512]{1,0:T(8,128)(2,1)S(1)} %multiply_convert_fusion.1), channel_id=1, replica_groups=mesh['ep'=64,'kv'=4] {'kv'}, dimensions={1}, use_global_device_ids=true | all-gather | bytes 655360 | tf_op jit(solution)/shard_map/all_gather | solution.py:107
  61.6 0.9 fusion.60
  62.4 0.8 fusion.66
  63.2 63.1 %all_to_all.15 = bf16[64,8,2048]{2,1,0:T(8,128)(2,1)} all-to-all(bf16[64,8,2048]{2,1,0:T(8,128)(2,1)S(1)} %fusion.66), channel_id=1, replica_groups=mesh['ep'=64,'kv'=4] {'ep'}, dimensions={0} | all-to-all | bytes 4194304 | tf_op jit(solution)/shard_map/all_to_all | solution.py:122
  126.2 3.5 %fusion.15 = f32[512,256]{1,0:T(8,128)} fusion(bf16[64,8,2048]{2,1,0:T(8,128)(2,1)} %all_to_all.15, bf16[4,2048,256]{2,1,0:T(8,128)(2,1)} %all-gather.7.cloned.1.call-done), kind=kOutput, calls=%fused_computation.18 | convolution fusion | flops 536870912 | bytes 3670016 | tf_op jit(solution)/shard_map/dot_general | solution.py:126
  129.8 2.9 fusion.11
  132.7 1.6 fusion.7
  134.3 1.5 fusion.19
  135.8 39.3 %all-gather.11.cloned.1.call-done = bf16[4,256,2048]{2,1,0:T(8,128)(2,1)} async-done(((bf16[1,256,2048]{2,1,0:T(8,128)(2,1)}), bf16[4,256,2048]{2,1,0:T(8,128)(2,1)}) %all-gather.11.cloned.1.call-update) | async-done | bytes 4194320 | tf_op jit(solution)/shard_map/all_gather | solution.py:53
  175.1 6.6 %fusion.46 = f32[512,2048]{1,0:T(8,128)} fusion(bf16[64,8,2048]{2,1,0:T(8,128)(2,1)} %all_to_all.15, bf16[4,256,2048]{2,1,0:T(8,128)(2,1)} %all-gather.11.cloned.1.call-done, bf16[4,2048,256]{2,1,0:T(8,128)(2,1)} %all-gather.9.cloned.1.call-done, f32[512,256]{1,0:T(8,128)} %fusion.19), kind=kOutput, calls=%fused_computation.33 | convolution fusion | flops 1074528256 | bytes 8912896 | tf_op jit(solution)/shard_map/dot_general | solution.py:129
  181.7 6.6 %fusion.52 = f32[512,2048]{1,0:T(8,128)} fusion(bf16[64,8,2048]{2,1,0:T(8,128)(2,1)} %all_to_all.15, bf16[4,256,2048]{2,1,0:T(8,128)(2,1)} %all-gather.11.cloned.1.call-done, bf16[4,2048,256]{2,1,0:T(8,128)(2,1)} %all-gather.9.cloned.1.call-done, f32[512,256]{1,0:T(8,128)} %fusion.11), kind=kOutput, calls=%fused_computation.35 | convolution fusion | flops 1074528256 | bytes 8912896 | tf_op jit(solution)/shard_map/dot_general | solution.py:129
  188.3 6.6 %fusion.49 = f32[512,2048]{1,0:T(8,128)} fusion(bf16[64,8,2048]{2,1,0:T(8,128)(2,1)} %all_to_all.15, bf16[4,256,2048]{2,1,0:T(8,128)(2,1)} %all-gather.11.cloned.1.call-done, bf16[4,2048,256]{2,1,0:T(8,128)(2,1)} %all-gather.9.cloned.1.call-done, f32[512,256]{1,0:T(8,128)} %fusion.15), kind=kOutput, calls=%fused_computation.34 | convolution fusion | flops 1074528256 | bytes 8912896 | tf_op jit(solution)/shard_map/dot_general | solution.py:129
  194.8 9.6 %fusion.2 = bf16[64,8,2048]{2,1,0:T(8,128)(2,1)} fusion(f32[512,2048]{1,0:T(8,128)} %fusion.52, f32[512,2048]{1,0:T(8,128)} %fusion.46, f32[512,2048]{1,0:T(8,128)} %fusion.49, bf16[4,256,2048]{2,1,0:T(8,128)(2,1)} %all-gather.11.cloned.1.call-done, bf16[64,8,2048]{2,1,0:T(8,128)(2,1)} %all_to_all.15, ...), kind=kOutput, calls=%fused_computation.3 | convolution fusion | flops 1078722560 | bytes 19398656 | tf_op jit(solution)/shard_map/dot_general | solution.py:129
  204.5 10.8 %all-to-all-start.1 = ((bf16[64,8,2048]{2,1,0:T(8,128)(2,1)}), bf16[64,8,2048]{2,1,0:T(8,128)(2,1)}, u32[]{:S(2)}, u32[]{:S(2)}) async-start(bf16[64,8,2048]{2,1,0:T(8,128)(2,1)} %fusion.2), calls=%async_computation.1 | async-start | bytes 4194304 | tf_op jit(solution)/shard_map/all_to_all | solution.py:131
  215.4 0.6 fusion.129
  216.0 50.5 %all-to-all-done.1 = bf16[64,8,2048]{2,1,0:T(8,128)(2,1)} async-done(((bf16[64,8,2048]{2,1,0:T(8,128)(2,1)}), bf16[64,8,2048]{2,1,0:T(8,128)(2,1)}, u32[]{:S(2)}, u32[]{:S(2)}) %all-to-all-start.1) | async-done | bytes 2097184 | tf_op jit(solution)/shard_map/all_to_all | solution.py:131
  266.5 2.1 convolution_bitcast_fusion
  268.7 2.1 fusion.4
  270.9 11.3 %all_to_all.16 = bf16[4,128,512]{2,1,0:T(8,128)(2,1)S(1)} all-to-all(bf16[4,128,512]{2,1,0:T(8,128)(2,1)S(1)} %bitcast.185), channel_id=1, replica_groups=mesh['ep'=64,'kv'=4] {'kv'}, dimensions={0} | all-to-all | bytes 1048576 | tf_op jit(solution)/shard_map/all_to_all | solution.py:139
  282.2 0.7 multiply_reduce_fusion
  283.0 8.9 %psum.7 = f32[128]{0:T(128)S(1)} all-reduce(f32[128]{0:T(128)S(1)} %get-tuple-element.7), channel_id=1, replica_groups=mesh['ep'=64,'kv'=4] {'kv'}, use_global_device_ids=true, to_apply=%region_14.15 | all-reduce | flops 128 | bytes 1024 | tf_op jit(solution)/shard_map/psum | solution.py:141
  291.9 1.7 multiply_convert_fusion
  (54 shorter events, 0.6 us)
Async XLA Ops:
  6.5 6.8 %copy-start = (bf16[6,128,2048]{2,1,0:T(8,128)(2,1)S(1)}, bf16[6,128,2048]{2,1,0:T(8,128)(2,1)}, u32[]{:S(2)}) copy-start(bf16[6,128,2048]{2,1,0:T(8,128)(2,1)} %param.17) | copy-start | bytes 9437188
  6.5 2.8 copy-start.10
  6.5 3.0 %copy-start.11 = (s32[2]{0:T(128)S(1)}, s32[2]{0:T(128)}, u32[]{:S(2)}) copy-start(s32[2]{0:T(128)} %param.19) | copy-start | bytes 28
  6.5 3.1 %copy-start.3 = (bf16[2,2048]{1,0:T(2,128)(2,1)S(1)}, bf16[2,2048]{1,0:T(2,128)(2,1)}, u32[]{:S(2)}) copy-start(bf16[2,2048]{1,0:T(2,128)(2,1)} %param.15) | copy-start | bytes 24580
  6.5 119.7 %all-gather.7.cloned.1.call-start = ((), (), s32[]{:S(2)}) async-start(), calls=%async_computation.3 | async-start | bytes 5242880 | tf_op jit(solution)/shard_map/all_gather | solution.py:51
  7.3 5.8 %copy-start.8 = (s32[128,8]{0,1:T(8,128)S(1)}, s32[128,8]{0,1:T(8,128)}, u32[]{:S(2)}) copy-start(s32[128,8]{0,1:T(8,128)} %param.29) | copy-start | bytes 12292
  7.3 128.5 %all-gather.9.cloned.1.call-start = ((), (), s32[]{:S(2)}) async-start(), calls=%async_computation.4 | async-start | bytes 5242880 | tf_op jit(solution)/shard_map/all_gather | solution.py:52
  8.0 167.0 %all-gather.11.cloned.1.call-start = ((), (), s32[]{:S(2)}) async-start(), calls=%async_computation.5 | async-start | bytes 5242880 | tf_op jit(solution)/shard_map/all_gather | solution.py:53
  13.1 14.1 %copy-start.6 = (s32[8]{0:T(128)}, s32[8]{0:T(128)S(1)}, u32[]{:S(2)}) copy-start(s32[8]{0:T(128)S(1)} %iota_add_fusion) | copy-start | bytes 100
  13.2 14.0 %copy-start.13 = (bf16[2048,512]{1,0:T(8,128)(2,1)S(1)}, bf16[2048,512]{1,0:T(8,128)(2,1)}, u32[]{:S(2)}) copy-start(bf16[2048,512]{1,0:T(8,128)(2,1)} %param.22) | copy-start | bytes 6291460
  13.2 14.0 %copy-start.14 = (bf16[126,2048]{1,0:T(8,128)(2,1)S(1)}, bf16[126,2048]{1,0:T(8,128)(2,1)}, u32[]{:S(2)}) copy-start(bf16[126,2048]{1,0:T(8,128)(2,1)} %param.20) | copy-start | bytes 1548292
  14.0 14.6 %copy-start.2 = (bf16[512,64]{0,1:T(8,128)(2,1)S(1)}, bf16[512,64]{0,1:T(8,128)(2,1)}, u32[]{:S(2)}) copy-start(bf16[512,64]{0,1:T(8,128)(2,1)} %param.24) | copy-start | bytes 196612
  14.0 14.6 %copy-start.4 = (f32[512]{0:T(512)S(1)}, f32[512]{0:T(512)}, u32[]{:S(2)}) copy-start(f32[512]{0:T(512)} %param.23) | copy-start | bytes 6148
  46.1 169.3 %copy-start.5 = (f32[128]{0:T(128)}, f32[128]{0:T(128)S(1)}, u32[]{:S(2)}) copy-start(f32[128]{0:T(128)S(1)} %fusion.140) | copy-start | bytes 1540
  126.2 3.5 %copy-start.1 = (bf16[64,8,2048]{2,1,0:T(8,128)(2,1)S(1)}, bf16[64,8,2048]{2,1,0:T(8,128)(2,1)}, u32[]{:S(2)}) copy-start(bf16[64,8,2048]{2,1,0:T(8,128)(2,1)} %all_to_all.15) | copy-start | bytes 6291460
  129.8 2.9 copy-start.12
  204.5 62.1 %copy-start.7 = (s32[8]{0:T(128)S(1)}, s32[8]{0:T(128)}, u32[]{:S(2)}) copy-start(s32[8]{0:T(128)} %copy-done.6) | copy-start | bytes 100
  204.5 62.0 %all-to-all-start.1 = ((bf16[64,8,2048]{2,1,0:T(8,128)(2,1)}), bf16[64,8,2048]{2,1,0:T(8,128)(2,1)}, u32[]{:S(2)}, u32[]{:S(2)}) async-start(bf16[64,8,2048]{2,1,0:T(8,128)(2,1)} %fusion.2), calls=%async_computation.1 | async-start | bytes 4194304 | tf_op jit(solution)/shard_map/all_to_all | solution.py:131
  268.7 23.2 %copy-start.9 = (f32[512]{0:T(512)S(1)}, f32[512]{0:T(512)}, u32[]{:S(2)}) copy-start(f32[512]{0:T(512)} %param.28) | copy-start | bytes 6148
Sparse Core Ops, SparseCore 0:
  9.2 59.7 all-gather.6
  70.8 51.2 all-gather.8
  123.9 51.1 all-gather.10

commit v2 on v1

v2 whole, which is shorter than its diff:
```python
import math

import jax
import jax.numpy as jnp
from jax import lax
from jax.experimental import pallas as pl
from jax.experimental.pallas import tpu as pltpu
from jax.sharding import PartitionSpec as P

HEAD_DIM = 128
TOP = 8

epsilon = 1e-06
floor_score = -1e30
MESH = pl.DeviceIdType.MESH


def split_two(v):
    high = v.astype(jnp.bfloat16)
    low = (v - high.astype(jnp.float32)).astype(jnp.bfloat16)
    return high, low


def iota(shape, axis):
    return lax.broadcasted_iota(jnp.int32, shape, axis)


def dot(a, b):
    return jnp.dot(a, b, preferred_element_type=jnp.float32)


def layer_kernel(
    n_ep,
    n_kv,
    queries,
    key_pool,
    value_pool,
    page_table,
    lengths,
    prefill,
    residual,
    w_out,
    norm_gain,
    router,
    w_gate,
    w_up,
    w_down,
    final_gain,
    routes_t,
    out,
    kbuf,
    vbuf,
    wobuf,
    attn,
    pack_all,
    stat_all,
    scaled_all,
    hidden,
    code_t,
    pick_t,
    sends,
    arrived,
    gates,
    ups,
    downs,
    total,
    replies,
    returned,
    part_out,
    part_in,
    square_all,
    load_sem,
    pack_sem,
    stat_sem,
    scaled_sem,
    weight_send,
    weight_recv,
    onward_send,
    onward_recv,
    out_sem,
    back_sem,
    part_sem,
    square_sem,
):
    me = lax.axis_index("ep")
    q = lax.axis_index("kv")
    rows, cols = hidden.shape
    width = cols * n_kv
    requests = queries.shape[0]
    heads = width // HEAD_DIM
    experts, share = sends.shape[0], sends.shape[1]
    tokens = kbuf.shape[0]
    page_rows = tokens // (requests * page_table.shape[2])

    def peer(d):
        return {"kv": lax.rem(q + d, n_kv)}

    loads = [
        pltpu.make_async_copy(key_pool, kbuf, load_sem.at[0]),
        pltpu.make_async_copy(value_pool, vbuf, load_sem.at[1]),
        pltpu.make_async_copy(w_out, wobuf, load_sem.at[2]),
        pltpu.make_async_copy(w_gate.at[0], gates.at[0], load_sem.at[3]),
        pltpu.make_async_copy(w_up.at[0], ups.at[0], load_sem.at[4]),
        pltpu.make_async_copy(w_down.at[0], downs.at[0], load_sem.at[5]),
    ]
    for load in loads:
        load.start()

    barrier = pltpu.get_barrier_semaphore()

    def greet(i, carry):
        pl.semaphore_signal(
            barrier, inc=1, device_id={"ep": lax.rem(me + i, n_ep)}, device_id_type=MESH
        )
        return carry

    lax.fori_loop(1, n_ep, greet, 0)
    for d in range(1, n_kv):
        pl.semaphore_signal(barrier, inc=1, device_id=peer(d), device_id_type=MESH)
    pl.semaphore_wait(barrier, n_ep - 1 + n_kv - 1)

    pairs = ((w_gate, gates), (w_up, ups), (w_down, downs))

    def half(ref, slot, side):
        size = ref.shape[1] // 2
        return ref.at[slot, pl.ds(side * size, size)]

    def ring_copy(w, way, side):
        source, target = pairs[w]
        return pltpu.make_async_remote_copy(
            src_ref=half(source, 0, side),
            dst_ref=half(target, 1 + way, side),
            send_sem=weight_send.at[w, way, side],
            recv_sem=weight_recv.at[w, way, side],
            device_id=peer(1 if way == 0 else n_kv - 1),
            device_id_type=MESH,
        )

    def onward_copy(w, way):
        target = pairs[w][1]
        return pltpu.make_async_remote_copy(
            src_ref=half(target, 1 + way, way),
            dst_ref=half(target, 3, way),
            send_sem=onward_send.at[w, way],
            recv_sem=onward_recv.at[w, way],
            device_id=peer(1 if way == 0 else n_kv - 1),
            device_id_type=MESH,
        )

    def start_weights():
        for w in range(3):
            for turn in range(2):
                for way in range(2):
                    ring_copy(w, way, way ^ turn).start()

    start_weights()

    on_head = iota((heads, width), 1) // HEAD_DIM == iota((heads, width), 0)
    spread = jnp.concatenate(
        [
            jnp.where(on_head, queries[r : r + 1, :].astype(jnp.float32), 0.0)
            for r in range(requests)
        ],
        axis=0,
    ).astype(jnp.bfloat16)
    lane = iota((heads, tokens), 1)
    page_of, in_page = lane // page_rows, lane % page_rows
    seen = []
    for r in range(requests):
        place = jnp.full((heads, tokens), 1 << 30, jnp.int32)
        for j in range(page_table.shape[2]):
            first = (j * n_kv + q) * page_rows
            place = jnp.where(page_of == page_table[r, 0, j], first + in_page, place)
        seen.append((place < lengths[r]).astype(jnp.int32))
    visible = jnp.concatenate(seen, axis=0) > 0
    loads[0].wait()
    scores = lax.dot_general(
        spread, kbuf[...], (((1,), (1,)), ((), ())), preferred_element_type=jnp.float32
    ) * (1.0 / math.sqrt(HEAD_DIM))
    masked = jnp.where(visible, scores, floor_score)
    peak = jnp.max(masked, axis=1, keepdims=True)
    weights = jnp.where(visible, jnp.exp(masked - peak), 0.0)
    mass = jnp.sum(weights, axis=1, keepdims=True)
    high, low = split_two(weights)
    loads[1].wait()
    wide = dot(high, vbuf[...]) + dot(low, vbuf[...])

    def on_lanes(values, r):
        part = jnp.broadcast_to(values[r * heads : (r + 1) * heads], (heads, width))
        return jnp.sum(jnp.where(on_head, part, 0.0), axis=0, keepdims=True)

    for r in range(requests):
        for i, item in enumerate((wide, peak, mass)):
            pack_all[q, i * requests + r : i * requests + r + 1, :] = on_lanes(item, r)

    def exchange(ref, sems):
        copies = []
        for d in range(1, n_kv):
            copies.append(
                pltpu.make_async_remote_copy(
                    src_ref=ref.at[q],
                    dst_ref=ref.at[q],
                    send_sem=sems.at[0, d - 1],
                    recv_sem=sems.at[1, d - 1],
                    device_id=peer(d),
                    device_id_type=MESH,
                )
            )
            copies[-1].start()
        return copies

    pack_copies = exchange(pack_all, pack_sem)

    expert_of = iota((experts, rows), 0)
    named = jnp.zeros((experts, rows), jnp.float32)
    for k in range(TOP):
        named = jnp.where(expert_of == routes_t[k : k + 1, :], 1.0, named)
    before = (iota((rows, rows), 0) < iota((rows, rows), 1)).astype(jnp.float32)
    rank = dot(named.astype(jnp.bfloat16), before.astype(jnp.bfloat16))
    code_t[...] = jnp.where(named > 0, rank, -1.0).astype(jnp.int32)
    slot = q * share + iota((experts, share, rows), 1)
    pick = (code_t[...][:, None, :] == slot).astype(jnp.float32).reshape(experts * share, rows)
    pick_t[...] = pick.astype(jnp.bfloat16)

    loads[2].wait()
    attn[0 : prefill.shape[0], :] = prefill[...]
    for copy in pack_copies:
        copy.wait()
    packs = pack_all[...]
    sums = packs[:, 0:requests]
    peaks = packs[:, requests : 2 * requests]
    masses = packs[:, 2 * requests : 3 * requests]
    factors = jnp.exp(peaks - jnp.max(peaks, axis=0)[None])
    attn[prefill.shape[0] :, :] = (
        jnp.sum(sums * factors, axis=0) / jnp.sum(masses * factors, axis=0)
    ).astype(jnp.bfloat16)
    state = residual[...].astype(jnp.float32) + dot(attn[...], wobuf[...])
    hidden[...] = state
    scaled = (state * norm_gain[...]).astype(jnp.bfloat16)
    scaled_all[q] = scaled
    squares = jnp.sum(state * state, axis=1, keepdims=True)
    stat_all[q] = jnp.concatenate(
        [
            dot(scaled, router[...]),
            jnp.broadcast_to(squares, (rows, 128 - experts)),
        ],
        axis=1,
    )
    stat_copies = exchange(stat_all, stat_sem)
    scaled_copies = exchange(scaled_all, scaled_sem)
    for copy in stat_copies:
        copy.wait()
    stats = stat_all[0]
    for j in range(1, n_kv):
        stats = stats + stat_all[j]
    inv_first = lax.rsqrt(stats[:, experts : experts + 1] / width + epsilon)
    logits_t = (stats * inv_first).T[0:experts, :]
    raised = jnp.where(code_t[...] >= 0, jnp.exp(logits_t), 0.0)
    gate_t = raised / jnp.sum(raised, axis=0, keepdims=True)
    for copy in scaled_copies:
        copy.wait()
    for j in range(n_kv):
        normed = (scaled_all[j].astype(jnp.float32) * inv_first).astype(jnp.bfloat16)
        picked = dot(pick_t[...], normed).reshape(experts, share, cols)
        sends[:, :, j * cols : (j + 1) * cols] = picked.astype(jnp.bfloat16)

    def all_to_all(source, target, sems):
        def send(i, carry):
            other = lax.rem(me + i, n_ep)
            pltpu.make_async_remote_copy(
                src_ref=source.at[other],
                dst_ref=target.at[me],
                send_sem=sems.at[0],
                recv_sem=sems.at[1],
                device_id={"ep": other},
                device_id_type=MESH,
            ).start()
            return carry

        lax.fori_loop(1, n_ep, send, 0)
        own = pltpu.make_async_copy(source.at[me], target.at[me], sems.at[2])
        own.start()

        def finish():
            own.wait()
            rest = source.at[pl.ds(0, n_ep - 1)]
            pltpu.make_async_copy(rest, rest, sems.at[0]).wait()
            pltpu.make_async_copy(rest, rest, sems.at[1]).wait()

        return finish

    finish_out = all_to_all(sends, arrived, out_sem)

    for w in range(3):
        for way in range(2):
            ring_copy(w, way, way).wait_recv()
            onward_copy(w, way).start()
    mix_high, mix_low = split_two(
        (
            jnp.broadcast_to(gate_t[:, None, :], (experts, share, rows))
            .reshape(experts * share, rows)
            * pick_t[...].astype(jnp.float32)
        ).T
    )
    for w in range(3):
        loads[3 + w].wait()
        for way in range(2):
            ring_copy(w, way, 1 - way).wait_recv()

    finish_out()

    tile_blocks = 32
    tile_rows = tile_blocks * share
    wide_cols = 512

    def chunk(c):
        def tile(m, carry):
            block = pl.multiple_of(m * tile_blocks, tile_blocks)
            row = pl.multiple_of(m * tile_rows, tile_rows)
            x = arrived[pl.ds(block, tile_blocks)].reshape(tile_rows, width)
            g = dot(x, gates[c])
            u = dot(x, ups[c])
            act = (g / (1.0 + jnp.exp(-g)) * u).astype(jnp.bfloat16)
            for n in range(width // wide_cols):
                span = pl.ds(n * wide_cols, wide_cols)
                term = dot(act, downs[c, :, span])
                if c > 0:
                    term = term + total[pl.ds(row, tile_rows), span]
                if c < n_kv - 1:
                    total[pl.ds(row, tile_rows), span] = term
                else:
                    replies[pl.ds(block, tile_blocks), :, span] = term.reshape(
                        tile_blocks, share, wide_cols
                    ).astype(jnp.bfloat16)
            return carry

        lax.fori_loop(0, n_ep // tile_blocks, tile, 0)

    for c in range(n_kv - 1):
        chunk(c)
    for w in range(3):
        for way in range(2):
            onward_copy(w, way).wait_recv()
    chunk(n_kv - 1)

    finish_back = all_to_all(replies, returned, back_sem)
    for w in range(3):
        for way in range(2):
            for side in range(2):
                ring_copy(w, way, side).wait_send()
            onward_copy(w, way).wait_send()
    finish_back()

    for j in range(n_kv):
        span = pl.ds(j * cols, cols)
        back = returned[:, :, span].reshape(experts * share, cols)
        part_out[j] = (dot(mix_high, back) + dot(mix_low, back)).astype(jnp.bfloat16)
    part_copies = []
    for d in range(1, n_kv):
        part_copies.append(
            pltpu.make_async_remote_copy(
                src_ref=part_out.at[lax.rem(q + d, n_kv)],
                dst_ref=part_in.at[d - 1],
                send_sem=part_sem.at[0, d - 1],
                recv_sem=part_sem.at[1, d - 1],
                device_id=peer(d),
                device_id_type=MESH,
            )
        )
        part_copies[-1].start()
    combined = hidden[...] + part_out[q].astype(jnp.float32)
    for copy in part_copies:
        copy.wait()
    for d in range(1, n_kv):
        combined = combined + part_in[d - 1].astype(jnp.float32)
    own_square = jnp.sum(combined * combined, axis=1, keepdims=True)
    square_all[q] = jnp.broadcast_to(own_square, (rows, 128))
    for copy in exchange(square_all, square_sem):
        copy.wait()
    square = square_all[0]
    for j in range(1, n_kv):
        square = square + square_all[j]
    inv_second = lax.rsqrt(square[:, 0:1] / width + epsilon)
    out[...] = (combined * inv_second * final_gain[...]).astype(out.dtype)


def make_per_device(n_ep, n_kv):
    def per_device(
        queries,
        key_pool,
        value_pool,
        page_table,
        lengths,
        prefill_attn,
        residual,
        w_out,
        norm_gain,
        router,
        w_gate,
        w_up,
        w_down,
        final_gain,
        routes,
    ):
        width = queries.shape[1]
        rows, cols = residual.shape
        experts = router.shape[1]
        share = min(rows, 2 * rows * TOP // experts) // n_kv
        tokens = key_pool.shape[0] * key_pool.shape[1]
        packed = 3 * queries.shape[0]
        f32, bf16 = jnp.float32, jnp.bfloat16
        vmem = pl.BlockSpec(memory_space=pltpu.VMEM)
        smem = pl.BlockSpec(memory_space=pltpu.SMEM)
        anywhere = pl.BlockSpec(memory_space=pl.ANY)
        dma = pltpu.SemaphoreType.DMA
        return pl.pallas_call(
            lambda *refs: layer_kernel(n_ep, n_kv, *refs),
            name="layer",
            out_shape=jax.ShapeDtypeStruct((rows, cols), bf16),
            in_specs=[vmem, anywhere, anywhere, smem, smem, vmem, vmem, anywhere, vmem, vmem]
            + [anywhere] * 3
            + [vmem, vmem],
            out_specs=vmem,
            scratch_shapes=[
                pltpu.VMEM((tokens, width), bf16),
                pltpu.VMEM((tokens, width), bf16),
                pltpu.VMEM(w_out.shape, bf16),
                pltpu.VMEM((rows, width), bf16),
                pltpu.VMEM((n_kv, packed, width), f32),
                pltpu.VMEM((n_kv, rows, 128), f32),
                pltpu.VMEM((n_kv, rows, cols), bf16),
                pltpu.VMEM((rows, cols), f32),
                pltpu.VMEM((experts, rows), jnp.int32),
                pltpu.VMEM((experts * share, rows), bf16),
                pltpu.VMEM((experts, share, width), bf16),
                pltpu.VMEM((experts, share, width), bf16),
                pltpu.VMEM((n_kv,) + w_gate.shape[1:], bf16),
                pltpu.VMEM((n_kv,) + w_up.shape[1:], bf16),
                pltpu.VMEM((n_kv,) + w_down.shape[1:], bf16),
                pltpu.VMEM((experts * share, width), f32),
                pltpu.VMEM((experts, share, width), bf16),
                pltpu.VMEM((experts, share, width), bf16),
                pltpu.VMEM((n_kv, rows, cols), bf16),
                pltpu.VMEM((n_kv - 1, rows, cols), bf16),
                pltpu.VMEM((n_kv, rows, 128), f32),
                dma((6,)),
                dma((2, n_kv - 1)),
                dma((2, n_kv - 1)),
                dma((2, n_kv - 1)),
                dma((3, 2, 2)),
                dma((3, 2, 2)),
                dma((3, 2)),
                dma((3, 2)),
                dma((3,)),
                dma((3,)),
                dma((2, n_kv - 1)),
                dma((2, n_kv - 1)),
            ],
            compiler_params=pltpu.CompilerParams(
                collective_id=0, has_side_effects=True, vmem_limit_bytes=60 << 20
            ),
        )(
            queries,
            key_pool.reshape(tokens, width),
            value_pool.reshape(tokens, width),
            page_table,
            lengths,
            prefill_attn,
            residual,
            w_out,
            norm_gain.reshape(1, cols),
            router,
            w_gate,
            w_up,
            w_down,
            final_gain.reshape(1, cols),
            routes.T,
        )

    return per_device


def solution(mesh):
    placed = (
        P("ep", None),
        P(("ep", "kv"), None, None),
        P(("ep", "kv"), None, None),
        P("ep", "kv", None),
        P("ep"),
        P("ep", None),
        P("ep", "kv"),
        P(None, "kv"),
        P("kv"),
        P("kv", None),
        P("ep", None, "kv"),
        P("ep", None, "kv"),
        P("ep", "kv", None),
        P("kv"),
        P("ep", None),
    )
    return jax.shard_map(
        make_per_device(mesh.shape["ep"], mesh.shape["kv"]),
        mesh=mesh,
        in_specs=placed,
        out_specs=P("ep", "kv"),
        check_vma=False,
    )
```

time: 301 us -> 222 us (0.74)
  Pallas kernels: 0 us -> 219 us
  blocking collectives: 125 us -> 0 us
  waiting for transfers between devices: 91.9 us -> 0 us
  matrix products: 50.1 us -> 0 us
  between operations: 13.4 us -> 0.01 us
  starting transfers between devices: 10.9 us -> 0 us
  other arithmetic: 5.8 us -> 0 us
    pallas_call x0 -> x1, Pallas kernels: none -> 219 us  [per_device(): pl.pallas_call(lambda *refs: layer_kernel(n_ep, n_kv, *refs), name='layer...]
    all_to_all x2 -> x0, blocking collectives: 74.3 us -> none  [the longest x1 63.1 us: per_device(): lax.all_to_all(outbound, 'ep', split_axis=0, concat_axis=0, tiled=True)]
    all_to_all x1 -> x0, waiting for transfers between devices: 50.5 us -> none  [per_device(): lax.all_to_all(expert_out, 'ep', split_axis=0, concat_axis=0, tiled=True)]
    dot_general x16 -> x0, matrix products: 50.1 us -> none  [the longest x4 29.4 us: per_device(): jnp.dot(activation, down_all[part], preferred_element_type=jnp.float32)]
    all_gather x3 -> x0, blocking collectives: 42.3 us -> none  [the longest x1 15.4 us: per_device(): full_rows = lax.all_gather(normed, 'kv', axis=1, tiled=True)]
    all_gather x3 -> x0, waiting for transfers between devices: 39.3 us -> none  [the longest x1 39.3 us: per_device(): down_all = lax.all_gather(w_down[0], 'kv', axis=0)]
    all_to_all x1 -> x0, starting transfers between devices: 10.8 us -> none  [per_device(): lax.all_to_all(expert_out, 'ep', split_axis=0, concat_axis=0, tiled=True)]
    psum x1 -> x0, blocking collectives: 8.87 us -> none  [per_device(): square_two = lax.psum(jnp.sum(combined * combined, axis=1), 'kv')]
  transfers between devices with their start and end apart: 4 -> 0, of which waited for: 2 -> 0; matrix products, arithmetic and copies ran while one was open for 7% -> 0% of each run, Pallas kernels for 0% -> 0%
where the time goes in v2:
time: 222 us
  Pallas kernels  219 us (99%)
  local copies, waits for them, and re-layouts  3.17 us (1%)
    pallas_call x1, Pallas kernels, per_device(): pl.pallas_call(lambda *refs: layer_kernel(n_ep, n_kv, *refs), name='layer...  219 us

profile of v2, /device:TPU:24, one launch (start us, length us, event | category | flops | bytes accessed | tf_op | source)
XLA Modules:
  0.0 222.3 jit_solution(10358732894754922568)
XLA Ops:
  0.0 1.6 copy.16.refs_9_
  1.6 219.1 %layer.1 = bf16[128,512]{1,0:T(8,128)(2,1)} custom-call(bf16[2,2048]{1,0:T(2,128)(2,1)} %refs_0_.1, bf16[768,2048]{1,0:T(8,128)(2,1)} %bitcast.5, bf16[768,2048]{1,0:T(8,128)(2,1)} %bitcast.6, s32[2,1,3]{2,1,0:T(1,128)} %refs_3_.1, s32[2]{0:T(128)} %refs_4_.1, bf16[126,2048]{1,0:T(8,128)(2,1)} %refs_5_.1, bf16[128,512]{1,0:T(8,128)(2,1)} %refs_6_.1, ...), custom_call_target="tpu_custom_call" | custom-call | tf_op jit(solution)/shard_map/layer/pallas_call | solution.py:416
  220.7 1.6 copy.18

commit v3 on v2

--- a/solution.py
+++ b/solution.py
@@ -13,6 +13,7 @@
 epsilon = 1e-06
 floor_score = -1e30
 MESH = pl.DeviceIdType.MESH
+PACE = (1, 2)
 
 
 def split_two(v):
@@ -41,7 +42,7 @@
     residual,
     w_out,
     norm_gain,
-    router,
+    router_t,
     w_gate,
     w_up,
     w_down,
@@ -63,7 +64,7 @@
     gates,
     ups,
     downs,
-    total,
+    acts,
     replies,
     returned,
     part_out,
@@ -73,10 +74,10 @@
     pack_sem,
     stat_sem,
     scaled_sem,
-    weight_send,
-    weight_recv,
-    onward_send,
-    onward_recv,
+    weight_sem,
+    onward_sem,
+    down_sem,
+    down_onward_sem,
     out_sem,
     back_sem,
     part_sem,
@@ -88,7 +89,7 @@
     width = cols * n_kv
     requests = queries.shape[0]
     heads = width // HEAD_DIM
-    experts, share = sends.shape[0], sends.shape[1]
+    experts, share = sends.shape[1], sends.shape[2]
     tokens = kbuf.shape[0]
     page_rows = tokens // (requests * page_table.shape[2])
 
@@ -117,43 +118,6 @@
     lax.fori_loop(1, n_ep, greet, 0)
     for d in range(1, n_kv):
         pl.semaphore_signal(barrier, inc=1, device_id=peer(d), device_id_type=MESH)
-    pl.semaphore_wait(barrier, n_ep - 1 + n_kv - 1)
-
-    pairs = ((w_gate, gates), (w_up, ups), (w_down, downs))
-
-    def half(ref, slot, side):
-        size = ref.shape[1] // 2
-        return ref.at[slot, pl.ds(side * size, size)]
-
-    def ring_copy(w, way, side):
-        source, target = pairs[w]
-        return pltpu.make_async_remote_copy(
-            src_ref=half(source, 0, side),
-            dst_ref=half(target, 1 + way, side),
-            send_sem=weight_send.at[w, way, side],
-            recv_sem=weight_recv.at[w, way, side],
-            device_id=peer(1 if way == 0 else n_kv - 1),
-            device_id_type=MESH,
-        )
-
-    def onward_copy(w, way):
-        target = pairs[w][1]
-        return pltpu.make_async_remote_copy(
-            src_ref=half(target, 1 + way, way),
-            dst_ref=half(target, 3, way),
-            send_sem=onward_send.at[w, way],
-            recv_sem=onward_recv.at[w, way],
-            device_id=peer(1 if way == 0 else n_kv - 1),
-            device_id_type=MESH,
-        )
-
-    def start_weights():
-        for w in range(3):
-            for turn in range(2):
-                for way in range(2):
-                    ring_copy(w, way, way ^ turn).start()
-
-    start_weights()
 
     on_head = iota((heads, width), 1) // HEAD_DIM == iota((heads, width), 0)
     spread = jnp.concatenate(
@@ -193,6 +157,8 @@
         for i, item in enumerate((wide, peak, mass)):
             pack_all[q, i * requests + r : i * requests + r + 1, :] = on_lanes(item, r)
 
+    pl.semaphore_wait(barrier, n_ep - 1 + n_kv - 1)
+
     def exchange(ref, sems):
         copies = []
         for d in range(1, n_kv):
@@ -210,6 +176,68 @@
         return copies
 
     pack_copies = exchange(pack_all, pack_sem)
+
+    pairs = ((w_gate, gates), (w_up, ups))
+    piece = gates.shape[1] // 4
+    down_rows = downs.shape[1] // 2
+
+    def neighbour(way):
+        return peer(1 if way == 0 else n_kv - 1)
+
+    def ring_copy(w, way, part):
+        source, target = pairs[w]
+        return pltpu.make_async_remote_copy(
+            src_ref=source.at[0, pl.ds(part * piece, piece)],
+            dst_ref=target.at[1 + way, pl.ds(part * piece, piece)],
+            send_sem=weight_sem.at[0, w, way, part],
+            recv_sem=weight_sem.at[1, w, way, part],
+            device_id=neighbour(way),
+            device_id_type=MESH,
+        )
+
+    def onward_copy(w, way, k):
+        target = pairs[w][1]
+        span = pl.ds((2 * way + k) * piece, piece)
+        return pltpu.make_async_remote_copy(
+            src_ref=target.at[1 + way, span],
+            dst_ref=target.at[3, span],
+            send_sem=onward_sem.at[0, w, way, k],
+            recv_sem=onward_sem.at[1, w, way, k],
+            device_id=neighbour(way),
+            device_id_type=MESH,
+        )
+
+    def down_copy(n, way):
+        span = pl.ds(n * cols, cols)
+        return pltpu.make_async_remote_copy(
+            src_ref=w_down.at[0, :, span],
+            dst_ref=downs.at[1 + way, :, span],
+            send_sem=down_sem.at[0, n, way],
+            recv_sem=down_sem.at[1, n, way],
+            device_id=neighbour(way),
+            device_id_type=MESH,
+        )
+
+    def down_onward(n, way):
+        span = pl.ds(n * cols, cols)
+        some = pl.ds(way * down_rows, down_rows)
+        return pltpu.make_async_remote_copy(
+            src_ref=downs.at[1 + way, some, span],
+            dst_ref=downs.at[3, some, span],
+            send_sem=down_onward_sem.at[0, n, way],
+            recv_sem=down_onward_sem.at[1, n, way],
+            device_id=neighbour(way),
+            device_id_type=MESH,
+        )
+
+    steps = [(w, k) for w in range(2) for k in range(4)]
+
+    def start_steps(first, last):
+        for w, k in steps[first:last]:
+            for way in range(2):
+                ring_copy(w, way, (k + 2 * way) % 4).start()
+
+    start_steps(0, PACE[0])
 
     expert_of = iota((experts, rows), 0)
     named = jnp.zeros((experts, rows), jnp.float32)
@@ -239,30 +267,21 @@
     scaled = (state * norm_gain[...]).astype(jnp.bfloat16)
     scaled_all[q] = scaled
     squares = jnp.sum(state * state, axis=1, keepdims=True)
-    stat_all[q] = jnp.concatenate(
-        [
-            dot(scaled, router[...]),
-            jnp.broadcast_to(squares, (rows, 128 - experts)),
-        ],
-        axis=1,
+    scores_of = lax.dot_general(
+        scaled, router_t[...], (((1,), (1,)), ((), ())), preferred_element_type=jnp.float32
     )
+    stat = jnp.concatenate([scores_of, jnp.broadcast_to(squares, (rows, 128 - experts))], axis=1)
+    stat_all[q] = stat.T[0 : stat_all.shape[1], :]
     stat_copies = exchange(stat_all, stat_sem)
     scaled_copies = exchange(scaled_all, scaled_sem)
+    start_steps(PACE[0], PACE[1])
     for copy in stat_copies:
         copy.wait()
     stats = stat_all[0]
     for j in range(1, n_kv):
         stats = stats + stat_all[j]
-    inv_first = lax.rsqrt(stats[:, experts : experts + 1] / width + epsilon)
-    logits_t = (stats * inv_first).T[0:experts, :]
-    raised = jnp.where(code_t[...] >= 0, jnp.exp(logits_t), 0.0)
-    gate_t = raised / jnp.sum(raised, axis=0, keepdims=True)
-    for copy in scaled_copies:
-        copy.wait()
-    for j in range(n_kv):
-        normed = (scaled_all[j].astype(jnp.float32) * inv_first).astype(jnp.bfloat16)
-        picked = dot(pick_t[...], normed).reshape(experts, share, cols)
-        sends[:, :, j * cols : (j + 1) * cols] = picked.astype(jnp.bfloat16)
+    inv_t = lax.rsqrt(stats[experts : experts + 1, :] / width + epsilon)
+    inv_first = jnp.broadcast_to(inv_t, (128, rows)).T[:, 0:1]
 
     def all_to_all(source, target, sems):
         def send(i, carry):
@@ -281,20 +300,40 @@
         own = pltpu.make_async_copy(source.at[me], target.at[me], sems.at[2])
         own.start()
 
-        def finish():
+        def received():
             own.wait()
+            rest = target.at[pl.ds(0, n_ep - 1)]
+            pltpu.make_async_copy(rest, rest, sems.at[1]).wait()
+
+        def sent():
             rest = source.at[pl.ds(0, n_ep - 1)]
             pltpu.make_async_copy(rest, rest, sems.at[0]).wait()
-            pltpu.make_async_copy(rest, rest, sems.at[1]).wait()
-
-        return finish
-
-    finish_out = all_to_all(sends, arrived, out_sem)
-
-    for w in range(3):
+
+        return received, sent
+
+    order = (0, 3, 1, 2)
+    out_waits = []
+    for i, off in enumerate(order):
+        if i > 0:
+            scaled_copies[n_kv - off - 1].wait()
+        quarter = scaled_all[lax.rem(q + off, n_kv)]
+        normed = (quarter.astype(jnp.float32) * inv_first).astype(jnp.bfloat16)
+        picked = dot(pick_t[...], normed).reshape(experts, share, cols)
+        sends[i] = picked.astype(jnp.bfloat16)
+        out_waits.append(all_to_all(sends.at[i], arrived.at[i], out_sem.at[i]))
+
+    start_steps(PACE[1], len(steps))
+    for w in range(2):
+        for k in range(2):
+            for way in range(2):
+                ring_copy(w, way, 2 * way + k).wait_recv()
+                onward_copy(w, way, k).start()
+    for n in range(2):
         for way in range(2):
-            ring_copy(w, way, way).wait_recv()
-            onward_copy(w, way).start()
+            down_copy(n, way).start()
+    logits_t = stats[0:experts, :] * inv_t
+    raised = jnp.where(code_t[...] >= 0, jnp.exp(logits_t), 0.0)
+    gate_t = raised / jnp.sum(raised, axis=0, keepdims=True)
     mix_high, mix_low = split_two(
         (
             jnp.broadcast_to(gate_t[:, None, :], (experts, share, rows))
@@ -304,83 +343,126 @@
     )
     for w in range(3):
         loads[3 + w].wait()
-        for way in range(2):
-            ring_copy(w, way, 1 - way).wait_recv()
-
-    finish_out()
+    for w in range(2):
+        for k in range(2):
+            for way in range(2):
+                ring_copy(w, way, 2 * (1 - way) + k).wait_recv()
+    for received, _ in out_waits:
+        received()
 
     tile_blocks = 32
     tile_rows = tile_blocks * share
-    wide_cols = 512
-
-    def chunk(c):
+
+    def expert_in(c):
         def tile(m, carry):
             block = pl.multiple_of(m * tile_blocks, tile_blocks)
             row = pl.multiple_of(m * tile_rows, tile_rows)
-            x = arrived[pl.ds(block, tile_blocks)].reshape(tile_rows, width)
-            g = dot(x, gates[c])
-            u = dot(x, ups[c])
-            act = (g / (1.0 + jnp.exp(-g)) * u).astype(jnp.bfloat16)
-            for n in range(width // wide_cols):
-                span = pl.ds(n * wide_cols, wide_cols)
-                term = dot(act, downs[c, :, span])
-                if c > 0:
-                    term = term + total[pl.ds(row, tile_rows), span]
-                if c < n_kv - 1:
-                    total[pl.ds(row, tile_rows), span] = term
-                else:
-                    replies[pl.ds(block, tile_blocks), :, span] = term.reshape(
-                        tile_blocks, share, wide_cols
-                    ).astype(jnp.bfloat16)
+            g = jnp.zeros((tile_rows, gates.shape[2]), jnp.float32)
+            u = jnp.zeros((tile_rows, gates.shape[2]), jnp.float32)
+            for i, off in enumerate(order):
+                x = arrived[i, pl.ds(block, tile_blocks)].reshape(tile_rows, cols)
+                some = pl.ds(pl.multiple_of(lax.rem(q + off, n_kv) * cols, cols), cols)
+                g = g + dot(x, gates[c, some, :])
+                u = u + dot(x, ups[c, some, :])
+            acts[c, pl.ds(row, tile_rows), :] = (g / (1.0 + jnp.exp(-g)) * u).astype(jnp.bfloat16)
             return carry
 
         lax.fori_loop(0, n_ep // tile_blocks, tile, 0)
 
+    def expert_out(n):
+        span = pl.ds(n * cols, cols)
+
+        def tile(m, carry):
+            block = pl.multiple_of(m * tile_blocks, tile_blocks)
+            row = pl.multiple_of(m * tile_rows, tile_rows)
+            term = jnp.zeros((tile_rows, cols), jnp.float32)
+            for c in range(n_kv):
+                term = term + dot(acts[c, pl.ds(row, tile_rows), :], downs[c, :, span])
+            replies[n, pl.ds(block, tile_blocks)] = term.reshape(
+                tile_blocks, share, cols
+            ).astype(jnp.bfloat16)
+            return carry
+
+        lax.fori_loop(0, n_ep // tile_blocks, tile, 0)
+
+    def advance(n):
+        for way in range(2):
+            down_copy(n, way).wait_recv()
+            down_onward(n, way).start()
+            if n + 2 < n_kv:
+                down_copy(n + 2, way).start()
+
     for c in range(n_kv - 1):
-        chunk(c)
-    for w in range(3):
+        expert_in(c)
+    advance(0)
+    for w in range(2):
+        for k in range(2):
+            for way in range(2):
+                onward_copy(w, way, k).wait_recv()
+    expert_in(n_kv - 1)
+    back_waits = []
+    for n in range(n_kv):
+        if n + 1 < n_kv:
+            advance(n + 1)
         for way in range(2):
-            onward_copy(w, way).wait_recv()
-    chunk(n_kv - 1)
-
-    finish_back = all_to_all(replies, returned, back_sem)
-    for w in range(3):
+            down_onward(n, way).wait_recv()
+        expert_out(n)
+        back_waits.append(all_to_all(replies.at[n], returned.at[n], back_sem.at[n]))
+    for _, sent in out_waits:
+        sent()
+    for w in range(2):
         for way in range(2):
-            for side in range(2):
-                ring_copy(w, way, side).wait_send()
-            onward_copy(w, way).wait_send()
-    finish_back()
-
-    for j in range(n_kv):
-        span = pl.ds(j * cols, cols)
-        back = returned[:, :, span].reshape(experts * share, cols)
-        part_out[j] = (dot(mix_high, back) + dot(mix_low, back)).astype(jnp.bfloat16)
-    part_copies = []
+            for part in range(4):
+                ring_copy(w, way, part).wait_send()
+            for k in range(2):
+                onward_copy(w, way, k).wait_send()
+    for n in range(n_kv):
+        for way in range(2):
+            down_copy(n, way).wait_send()
+            down_onward(n, way).wait_send()
+
+    def part_copy(n):
+        place = lax.rem(q - n + n_kv, n_kv) - 1
+        return pltpu.make_async_remote_copy(
+            src_ref=part_out.at[n],
+            dst_ref=part_in.at[place],
+            send_sem=part_sem.at[0, n],
+            recv_sem=part_sem.at[1, place],
+            device_id={"kv": n},
+            device_id_type=MESH,
+        )
+
+    for n in range(n_kv):
+        back_waits[n][0]()
+        back = returned[n].reshape(experts * share, cols)
+        part_out[n] = (dot(mix_high, back) + dot(mix_low, back)).astype(jnp.bfloat16)
+
+        @pl.when(q != n)
+        def _():
+            part_copy(n).start()
+
+    combined = hidden[...] + part_out[q].astype(jnp.float32)
     for d in range(1, n_kv):
-        part_copies.append(
-            pltpu.make_async_remote_copy(
-                src_ref=part_out.at[lax.rem(q + d, n_kv)],
-                dst_ref=part_in.at[d - 1],
-                send_sem=part_sem.at[0, d - 1],
-                recv_sem=part_sem.at[1, d - 1],
-                device_id=peer(d),
-                device_id_type=MESH,
-            )
-        )
-        part_copies[-1].start()
-    combined = hidden[...] + part_out[q].astype(jnp.float32)
-    for copy in part_copies:
-        copy.wait()
-    for d in range(1, n_kv):
+        pltpu.make_async_copy(part_in.at[d - 1], part_in.at[d - 1], part_sem.at[1, d - 1]).wait()
         combined = combined + part_in[d - 1].astype(jnp.float32)
     own_square = jnp.sum(combined * combined, axis=1, keepdims=True)
-    square_all[q] = jnp.broadcast_to(own_square, (rows, 128))
-    for copy in exchange(square_all, square_sem):
+    square_all[q] = jnp.broadcast_to(own_square, (rows, 128)).T[0:8, :]
+    square_copies = exchange(square_all, square_sem)
+    for _, sent in back_waits:
+        sent()
+    for n in range(n_kv):
+
+        @pl.when(q != n)
+        def _():
+            part_copy(n).wait_send()
+
+    for copy in square_copies:
         copy.wait()
     square = square_all[0]
     for j in range(1, n_kv):
         square = square + square_all[j]
-    inv_second = lax.rsqrt(square[:, 0:1] / width + epsilon)
+    inv_row = lax.rsqrt(square[0:1] / width + epsilon)
+    inv_second = jnp.broadcast_to(inv_row, (128, rows)).T[:, 0:1]
     out[...] = (combined * inv_second * final_gain[...]).astype(out.dtype)
 
 
@@ -427,33 +509,33 @@
                 pltpu.VMEM(w_out.shape, bf16),
                 pltpu.VMEM((rows, width), bf16),
                 pltpu.VMEM((n_kv, packed, width), f32),
-                pltpu.VMEM((n_kv, rows, 128), f32),
+                pltpu.VMEM((n_kv, experts + 8, rows), f32),
                 pltpu.VMEM((n_kv, rows, cols), bf16),
                 pltpu.VMEM((rows, cols), f32),
                 pltpu.VMEM((experts, rows), jnp.int32),
                 pltpu.VMEM((experts * share, rows), bf16),
-                pltpu.VMEM((experts, share, width), bf16),
-                pltpu.VMEM((experts, share, width), bf16),
+                pltpu.VMEM((n_kv, experts, share, cols), bf16),
+                pltpu.VMEM((n_kv, experts, share, cols), bf16),
                 pltpu.VMEM((n_kv,) + w_gate.shape[1:], bf16),
                 pltpu.VMEM((n_kv,) + w_up.shape[1:], bf16),
                 pltpu.VMEM((n_kv,) + w_down.shape[1:], bf16),
-                pltpu.VMEM((experts * share, width), f32),
-                pltpu.VMEM((experts, share, width), bf16),
-                pltpu.VMEM((experts, share, width), bf16),
+                pltpu.VMEM((n_kv, experts * share, w_gate.shape[2]), bf16),
+                pltpu.VMEM((n_kv, experts, share, cols), bf16),
+                pltpu.VMEM((n_kv, experts, share, cols), bf16),
                 pltpu.VMEM((n_kv, rows, cols), bf16),
                 pltpu.VMEM((n_kv - 1, rows, cols), bf16),
-                pltpu.VMEM((n_kv, rows, 128), f32),
+                pltpu.VMEM((n_kv, 8, rows), f32),
                 dma((6,)),
                 dma((2, n_kv - 1)),
                 dma((2, n_kv - 1)),
                 dma((2, n_kv - 1)),
-                dma((3, 2, 2)),
-                dma((3, 2, 2)),
-                dma((3, 2)),
-                dma((3, 2)),
-                dma((3,)),
-                dma((3,)),
-                dma((2, n_kv - 1)),
+                dma((2, 2, 2, 4)),
+                dma((2, 2, 2, 2)),
+                dma((2, n_kv, 2)),
+                dma((2, n_kv, 2)),
+                dma((n_kv, 3)),
+                dma((n_kv, 3)),
+                dma((2, n_kv)),
                 dma((2, n_kv - 1)),
             ],
             compiler_params=pltpu.CompilerParams(
@@ -469,7 +551,7 @@
             residual,
             w_out,
             norm_gain.reshape(1, cols),
-            router,
+            router.T,
             w_gate,
             w_up,
             w_down,

time: 222 us -> 170 us (0.77)
  Pallas kernels: 219 us -> 168 us
    pallas_call x1, Pallas kernels: 219 us -> 168 us  [per_device(): pl.pallas_call(lambda *refs: layer_kernel(n_ep, n_kv, *refs), name='layer...]
where the time goes in v3:
time: 170 us
  Pallas kernels  168 us (99%)
    pallas_call x1, Pallas kernels, per_device(): pl.pallas_call(lambda *refs: layer_kernel(n_ep, n_kv, *refs), name='layer...  168 us

profile of v3, /device:TPU:24, one launch (start us, length us, event | category | flops | bytes accessed | tf_op | source)
XLA Modules:
  0.0 169.6 jit_solution(5010232593930596978)
XLA Ops:
  0.0 168.0 %layer.1 = bf16[128,512]{1,0:T(8,128)(2,1)} custom-call(bf16[2,2048]{1,0:T(2,128)(2,1)} %refs_0_.1, bf16[768,2048]{1,0:T(8,128)(2,1)} %bitcast.6, bf16[768,2048]{1,0:T(8,128)(2,1)} %bitcast.7, s32[2,1,3]{2,1,0:T(1,128)} %refs_3_.1, s32[2]{0:T(128)} %refs_4_.1, bf16[126,2048]{1,0:T(8,128)(2,1)} %refs_5_.1, bf16[128,512]{1,0:T(8,128)(2,1)} %refs_6_.1, ...), custom_call_target="tpu_custom_call" | custom-call | tf_op jit(solution)/shard_map/layer/pallas_call | solution.py:498
  168.0 1.6 copy.17

commit v4 on v3

--- a/solution.py
+++ b/solution.py
@@ -13,7 +13,6 @@
 epsilon = 1e-06
 floor_score = -1e30
 MESH = pl.DeviceIdType.MESH
-PACE = (1, 2)
 
 
 def split_two(v):
@@ -74,10 +73,7 @@
     pack_sem,
     stat_sem,
     scaled_sem,
-    weight_sem,
-    onward_sem,
-    down_sem,
-    down_onward_sem,
+    ring_sem,
     out_sem,
     back_sem,
     part_sem,
@@ -96,16 +92,30 @@
     def peer(d):
         return {"kv": lax.rem(q + d, n_kv)}
 
+    side = q // 2
+    core = lax.rem(me, 2)
+    home = core == side
+    sibling = {"ep": me + 1 - 2 * core}
+    partner = {"kv": q + 1 - 2 * lax.rem(q, 2)}
+    across = {"kv": n_kv - 1 - q, "ep": me + 1 - 2 * core}
+
     loads = [
         pltpu.make_async_copy(key_pool, kbuf, load_sem.at[0]),
         pltpu.make_async_copy(value_pool, vbuf, load_sem.at[1]),
         pltpu.make_async_copy(w_out, wobuf, load_sem.at[2]),
+    ]
+    for load in loads:
+        load.start()
+    own_loads = [
         pltpu.make_async_copy(w_gate.at[0], gates.at[0], load_sem.at[3]),
         pltpu.make_async_copy(w_up.at[0], ups.at[0], load_sem.at[4]),
         pltpu.make_async_copy(w_down.at[0], downs.at[0], load_sem.at[5]),
     ]
-    for load in loads:
-        load.start()
+
+    @pl.when(home)
+    def _():
+        for load in own_loads:
+            load.start()
 
     barrier = pltpu.get_barrier_semaphore()
 
@@ -118,6 +128,7 @@
     lax.fori_loop(1, n_ep, greet, 0)
     for d in range(1, n_kv):
         pl.semaphore_signal(barrier, inc=1, device_id=peer(d), device_id_type=MESH)
+    pl.semaphore_signal(barrier, inc=1, device_id=across, device_id_type=MESH)
 
     on_head = iota((heads, width), 1) // HEAD_DIM == iota((heads, width), 0)
     spread = jnp.concatenate(
@@ -157,7 +168,7 @@
         for i, item in enumerate((wide, peak, mass)):
             pack_all[q, i * requests + r : i * requests + r + 1, :] = on_lanes(item, r)
 
-    pl.semaphore_wait(barrier, n_ep - 1 + n_kv - 1)
+    pl.semaphore_wait(barrier, n_ep - 1 + n_kv)
 
     def exchange(ref, sems):
         copies = []
@@ -177,76 +188,78 @@
 
     pack_copies = exchange(pack_all, pack_sem)
 
-    pairs = ((w_gate, gates), (w_up, ups))
     piece = gates.shape[1] // 4
-    down_rows = downs.shape[1] // 2
-
-    def neighbour(way):
-        return peer(1 if way == 0 else n_kv - 1)
-
-    def ring_copy(w, way, part):
-        source, target = pairs[w]
+    wide_items, items = 8, 12
+
+    def view(slot, t):
+        if t < wide_items:
+            return (gates, ups)[t // 4].at[slot, pl.ds(t % 4 * piece, piece)]
+        return downs.at[slot, :, pl.ds((t - wide_items) * cols, cols)]
+
+    def own_view(t):
+        if t < wide_items:
+            return (w_gate, w_up)[t // 4].at[0, pl.ds(t % 4 * piece, piece)]
+        return w_down.at[0, :, pl.ds((t - wide_items) * cols, cols)]
+
+    def move(kind, t):
+        source, slot, device = (
+            (own_view(t), 0, across),
+            (view(0, t), 1, partner),
+            (view(0, t), 2, sibling),
+            (view(1, t), 3, sibling),
+        )[kind]
         return pltpu.make_async_remote_copy(
-            src_ref=source.at[0, pl.ds(part * piece, piece)],
-            dst_ref=target.at[1 + way, pl.ds(part * piece, piece)],
-            send_sem=weight_sem.at[0, w, way, part],
-            recv_sem=weight_sem.at[1, w, way, part],
-            device_id=neighbour(way),
+            src_ref=source,
+            dst_ref=view(slot, t),
+            send_sem=ring_sem.at[0, kind, t],
+            recv_sem=ring_sem.at[1, kind, t],
+            device_id=device,
             device_id_type=MESH,
         )
 
-    def onward_copy(w, way, k):
-        target = pairs[w][1]
-        span = pl.ds((2 * way + k) * piece, piece)
-        return pltpu.make_async_remote_copy(
-            src_ref=target.at[1 + way, span],
-            dst_ref=target.at[3, span],
-            send_sem=onward_sem.at[0, w, way, k],
-            recv_sem=onward_sem.at[1, w, way, k],
-            device_id=neighbour(way),
-            device_id_type=MESH,
-        )
-
-    def down_copy(n, way):
-        span = pl.ds(n * cols, cols)
-        return pltpu.make_async_remote_copy(
-            src_ref=w_down.at[0, :, span],
-            dst_ref=downs.at[1 + way, :, span],
-            send_sem=down_sem.at[0, n, way],
-            recv_sem=down_sem.at[1, n, way],
-            device_id=neighbour(way),
-            device_id_type=MESH,
-        )
-
-    def down_onward(n, way):
-        span = pl.ds(n * cols, cols)
-        some = pl.ds(way * down_rows, down_rows)
-        return pltpu.make_async_remote_copy(
-            src_ref=downs.at[1 + way, some, span],
-            dst_ref=downs.at[3, some, span],
-            send_sem=down_onward_sem.at[0, n, way],
-            recv_sem=down_onward_sem.at[1, n, way],
-            device_id=neighbour(way),
-            device_id_type=MESH,
-        )
-
-    steps = [(w, k) for w in range(2) for k in range(4)]
-
-    def start_steps(first, last):
-        for w, k in steps[first:last]:
-            for way in range(2):
-                ring_copy(w, way, (k + 2 * way) % 4).start()
-
-    start_steps(0, PACE[0])
-
-    expert_of = iota((experts, rows), 0)
-    named = jnp.zeros((experts, rows), jnp.float32)
-    for k in range(TOP):
-        named = jnp.where(expert_of == routes_t[k : k + 1, :], 1.0, named)
+    def first_on(t):
+        move(1, t).start()
+        move(2, t).start()
+
+    def second_on(t):
+        move(1, t).wait_recv()
+        move(3, t).start()
+
+    def pump(home_items, cross_items, guest_items):
+        @pl.when(home)
+        def _():
+            for t in home_items:
+                first_on(t)
+
+        @pl.when(jnp.logical_not(home))
+        def _():
+            for t in cross_items:
+                move(0, t).start()
+            for t in guest_items:
+                move(0, t).wait_recv()
+                first_on(t)
+
+    @pl.when(home)
+    def _():
+        for load in own_loads:
+            load.wait()
+
+    pump(range(0, 1), range(0, 2), ())
+
+    def naming(expert_of):
+        named = jnp.zeros((experts, rows), jnp.float32)
+        for k in range(TOP):
+            named = jnp.where(expert_of == routes_t[k : k + 1, :], 1.0, named)
+        return named
+
+    device_of = iota((experts, rows), 0)
+    named = naming(device_of // 2 * 2 + side)
     before = (iota((rows, rows), 0) < iota((rows, rows), 1)).astype(jnp.float32)
     rank = dot(named.astype(jnp.bfloat16), before.astype(jnp.bfloat16))
     code_t[...] = jnp.where(named > 0, rank, -1.0).astype(jnp.int32)
-    slot = q * share + iota((experts, share, rows), 1)
+    slot = (lax.rem(q, 2) * 2 + iota((experts, share, rows), 0) % 2) * share + iota(
+        (experts, share, rows), 1
+    )
     pick = (code_t[...][:, None, :] == slot).astype(jnp.float32).reshape(experts * share, rows)
     pick_t[...] = pick.astype(jnp.bfloat16)
 
@@ -274,7 +287,7 @@
     stat_all[q] = stat.T[0 : stat_all.shape[1], :]
     stat_copies = exchange(stat_all, stat_sem)
     scaled_copies = exchange(scaled_all, scaled_sem)
-    start_steps(PACE[0], PACE[1])
+    pump(range(1, 3), range(2, 3), range(0, 1))
     for copy in stat_copies:
         copy.wait()
     stats = stat_all[0]
@@ -316,24 +329,27 @@
     for i, off in enumerate(order):
         if i > 0:
             scaled_copies[n_kv - off - 1].wait()
+        if i == n_kv - 1:
+            pump(range(3, 6), range(3, items), range(1, 3))
         quarter = scaled_all[lax.rem(q + off, n_kv)]
         normed = (quarter.astype(jnp.float32) * inv_first).astype(jnp.bfloat16)
         picked = dot(pick_t[...], normed).reshape(experts, share, cols)
         sends[i] = picked.astype(jnp.bfloat16)
         out_waits.append(all_to_all(sends.at[i], arrived.at[i], out_sem.at[i]))
 
-    start_steps(PACE[1], len(steps))
-    for w in range(2):
-        for k in range(2):
-            for way in range(2):
-                ring_copy(w, way, 2 * way + k).wait_recv()
-                onward_copy(w, way, k).start()
-    for n in range(2):
-        for way in range(2):
-            down_copy(n, way).start()
+    second_on(0)
+    for t in range(3, wide_items):
+        pump(range(t + 3, t + 4), (), range(t, t + 1))
+        second_on(t - 2)
+    pump(range(wide_items + 3, items), (), range(wide_items, wide_items + 2))
+    for t in range(wide_items - 2, wide_items):
+        second_on(t)
+    pump((), (), range(wide_items + 2, items))
     logits_t = stats[0:experts, :] * inv_t
-    raised = jnp.where(code_t[...] >= 0, jnp.exp(logits_t), 0.0)
-    gate_t = raised / jnp.sum(raised, axis=0, keepdims=True)
+    totals = jnp.sum(jnp.where(naming(device_of) > 0, jnp.exp(logits_t), 0.0), axis=0, keepdims=True)
+    turned = jnp.where(side == 0, pltpu.roll(logits_t, 1, 0), pltpu.roll(logits_t, experts - 1, 0))
+    served = jnp.where(device_of % 2 == side, logits_t, turned)
+    gate_t = jnp.where(code_t[...] >= 0, jnp.exp(served), 0.0) / totals
     mix_high, mix_low = split_two(
         (
             jnp.broadcast_to(gate_t[:, None, :], (experts, share, rows))
@@ -341,12 +357,6 @@
             * pick_t[...].astype(jnp.float32)
         ).T
     )
-    for w in range(3):
-        loads[3 + w].wait()
-    for w in range(2):
-        for k in range(2):
-            for way in range(2):
-                ring_copy(w, way, 2 * (1 - way) + k).wait_recv()
     for received, _ in out_waits:
         received()
 
@@ -385,41 +395,31 @@
 
         lax.fori_loop(0, n_ep // tile_blocks, tile, 0)
 
-    def advance(n):
-        for way in range(2):
-            down_copy(n, way).wait_recv()
-            down_onward(n, way).start()
-            if n + 2 < n_kv:
-                down_copy(n + 2, way).start()
-
-    for c in range(n_kv - 1):
+    for c in range(2):
         expert_in(c)
-    advance(0)
-    for w in range(2):
-        for k in range(2):
-            for way in range(2):
-                onward_copy(w, way, k).wait_recv()
-    expert_in(n_kv - 1)
+    for kind in range(2, 4):
+        for t in range(wide_items):
+            move(kind, t).wait_recv()
+        expert_in(kind)
+    second_on(wide_items)
     back_waits = []
     for n in range(n_kv):
         if n + 1 < n_kv:
-            advance(n + 1)
-        for way in range(2):
-            down_onward(n, way).wait_recv()
+            second_on(wide_items + n + 1)
+        for kind in range(2, 4):
+            move(kind, wide_items + n).wait_recv()
         expert_out(n)
         back_waits.append(all_to_all(replies.at[n], returned.at[n], back_sem.at[n]))
     for _, sent in out_waits:
         sent()
-    for w in range(2):
-        for way in range(2):
-            for part in range(4):
-                ring_copy(w, way, part).wait_send()
-            for k in range(2):
-                onward_copy(w, way, k).wait_send()
-    for n in range(n_kv):
-        for way in range(2):
-            down_copy(n, way).wait_send()
-            down_onward(n, way).wait_send()
+    for t in range(items):
+        for kind in range(1, 4):
+            move(kind, t).wait_send()
+
+    @pl.when(jnp.logical_not(home))
+    def _():
+        for t in range(items):
+            move(0, t).wait_send()
 
     def part_copy(n):
         place = lax.rem(q - n + n_kv, n_kv) - 1
@@ -529,10 +529,7 @@
                 dma((2, n_kv - 1)),
                 dma((2, n_kv - 1)),
                 dma((2, n_kv - 1)),
-                dma((2, 2, 2, 4)),
-                dma((2, 2, 2, 2)),
-                dma((2, n_kv, 2)),
-                dma((2, n_kv, 2)),
+                dma((2, 4, 12)),
                 dma((n_kv, 3)),
                 dma((n_kv, 3)),
                 dma((2, n_kv)),

time: 170 us -> 147 us (0.86)
  Pallas kernels: 168 us -> 144 us
    pallas_call x1, Pallas kernels: 168 us -> 144 us  [per_device(): pl.pallas_call(lambda *refs: layer_kernel(n_ep, n_kv, *refs), name='layer...]
where the time goes in v4:
time: 147 us; the launch traced here: 146 us
  Pallas kernels  144 us (98%)
  local copies, waits for them, and re-layouts  1.57 us (1%)
    pallas_call x1, Pallas kernels, per_device(): pl.pallas_call(lambda *refs: layer_kernel(n_ep, n_kv, *refs), name='layer...  144 us

profile of v4, /device:TPU:24, one launch (start us, length us, event | category | flops | bytes accessed | tf_op | source)
XLA Modules:
  0.0 145.9 jit_solution(13772554138709383350)
XLA Ops:
  0.0 144.3 %layer.1 = bf16[128,512]{1,0:T(8,128)(2,1)} custom-call(bf16[2,2048]{1,0:T(2,128)(2,1)} %refs_0_.1, bf16[768,2048]{1,0:T(8,128)(2,1)} %bitcast.6, bf16[768,2048]{1,0:T(8,128)(2,1)} %bitcast.7, s32[2,1,3]{2,1,0:T(1,128)} %refs_3_.1, s32[2]{0:T(128)} %refs_4_.1, bf16[126,2048]{1,0:T(8,128)(2,1)} %refs_5_.1, bf16[128,512]{1,0:T(8,128)(2,1)} %refs_6_.1, ...), custom_call_target="tpu_custom_call" | custom-call | tf_op jit(solution)/shard_map/layer/pallas_call | solution.py:498
  144.3 1.6 %copy.17 = bf16[128,512]{1,0:T(8,128)(2,1)} copy(bf16[128,512]{1,0:T(8,128)(2,1)} %layer.1) | data formatting | bytes 262144

commit v5 on v4

--- a/solution.py
+++ b/solution.py
@@ -63,6 +63,10 @@
     gates,
     ups,
     downs,
+    inv_out,
+    inv_in,
+    inv_wide,
+    total,
     acts,
     replies,
     returned,
@@ -74,6 +78,7 @@
     stat_sem,
     scaled_sem,
     ring_sem,
+    inv_sem,
     out_sem,
     back_sem,
     part_sem,
@@ -288,14 +293,6 @@
     stat_copies = exchange(stat_all, stat_sem)
     scaled_copies = exchange(scaled_all, scaled_sem)
     pump(range(1, 3), range(2, 3), range(0, 1))
-    for copy in stat_copies:
-        copy.wait()
-    stats = stat_all[0]
-    for j in range(1, n_kv):
-        stats = stats + stat_all[j]
-    inv_t = lax.rsqrt(stats[experts : experts + 1, :] / width + epsilon)
-    inv_first = jnp.broadcast_to(inv_t, (128, rows)).T[:, 0:1]
-
     def all_to_all(source, target, sems):
         def send(i, carry):
             other = lax.rem(me + i, n_ep)
@@ -326,17 +323,30 @@
 
     order = (0, 3, 1, 2)
     out_waits = []
-    for i, off in enumerate(order):
-        if i > 0:
-            scaled_copies[n_kv - off - 1].wait()
-        if i == n_kv - 1:
-            pump(range(3, 6), range(3, items), range(1, 3))
-        quarter = scaled_all[lax.rem(q + off, n_kv)]
-        normed = (quarter.astype(jnp.float32) * inv_first).astype(jnp.bfloat16)
-        picked = dot(pick_t[...], normed).reshape(experts, share, cols)
-        sends[i] = picked.astype(jnp.bfloat16)
+
+    def dispatch(i):
+        picked = dot(pick_t[...], scaled_all[lax.rem(q + order[i], n_kv)])
+        sends[i] = picked.reshape(experts, share, cols).astype(jnp.bfloat16)
         out_waits.append(all_to_all(sends.at[i], arrived.at[i], out_sem.at[i]))
 
+    dispatch(0)
+    for copy in stat_copies:
+        copy.wait()
+    stats = stat_all[0]
+    for j in range(1, n_kv):
+        stats = stats + stat_all[j]
+    inv_t = lax.rsqrt(stats[experts : experts + 1, :] / width + epsilon)
+    for copy in scaled_copies:
+        copy.wait()
+    pump(range(3, 6), range(3, items), range(1, 3))
+    for i in range(1, n_kv - 1):
+        dispatch(i)
+    on_lane = iota((experts, share, rows), 2) == iota((experts, share, rows), 1)
+    slot_pick = pick_t[...].astype(jnp.float32).reshape(experts, share, rows)
+    slot_inv = jnp.sum(slot_pick * inv_t[None], axis=2, keepdims=True)
+    inv_out[...] = jnp.sum(jnp.where(on_lane, slot_inv, 0.0), axis=1, keepdims=True)
+    inv_received, inv_sent = all_to_all(inv_out, inv_in, inv_sem)
+    dispatch(n_kv - 1)
     second_on(0)
     for t in range(3, wide_items):
         pump(range(t + 3, t + 4), (), range(t, t + 1))
@@ -357,24 +367,35 @@
             * pick_t[...].astype(jnp.float32)
         ).T
     )
-    for received, _ in out_waits:
-        received()
-
     tile_blocks = 32
     tile_rows = tile_blocks * share
 
-    def expert_in(c):
+    hidden_cols = gates.shape[2]
+
+    def expert_in(c, first, last):
         def tile(m, carry):
             block = pl.multiple_of(m * tile_blocks, tile_blocks)
             row = pl.multiple_of(m * tile_rows, tile_rows)
-            g = jnp.zeros((tile_rows, gates.shape[2]), jnp.float32)
-            u = jnp.zeros((tile_rows, gates.shape[2]), jnp.float32)
-            for i, off in enumerate(order):
+            if first == 0:
+                g = jnp.zeros((tile_rows, hidden_cols), jnp.float32)
+                u = jnp.zeros((tile_rows, hidden_cols), jnp.float32)
+            else:
+                g = total[c, 0, pl.ds(row, tile_rows), :]
+                u = total[c, 1, pl.ds(row, tile_rows), :]
+            for i in range(first, last):
+                off = order[i]
                 x = arrived[i, pl.ds(block, tile_blocks)].reshape(tile_rows, cols)
                 some = pl.ds(pl.multiple_of(lax.rem(q + off, n_kv) * cols, cols), cols)
                 g = g + dot(x, gates[c, some, :])
                 u = u + dot(x, ups[c, some, :])
-            acts[c, pl.ds(row, tile_rows), :] = (g / (1.0 + jnp.exp(-g)) * u).astype(jnp.bfloat16)
+            if last < n_kv:
+                total[c, 0, pl.ds(row, tile_rows), :] = g
+                total[c, 1, pl.ds(row, tile_rows), :] = u
+            else:
+                g = g * inv_wide[pl.ds(row, tile_rows), :]
+                u = u * inv_wide[pl.ds(row, tile_rows), :]
+                act = (g / (1.0 + jnp.exp(-g)) * u).astype(jnp.bfloat16)
+                acts[c, pl.ds(row, tile_rows), :] = act
             return carry
 
         lax.fori_loop(0, n_ep // tile_blocks, tile, 0)
@@ -395,12 +416,23 @@
 
         lax.fori_loop(0, n_ep // tile_blocks, tile, 0)
 
-    for c in range(2):
-        expert_in(c)
-    for kind in range(2, 4):
-        for t in range(wide_items):
-            move(kind, t).wait_recv()
-        expert_in(kind)
+    for i in range(n_kv - 1):
+        out_waits[i][0]()
+    for c in range(n_kv):
+        if c >= 2:
+            for t in range(wide_items):
+                move(c, t).wait_recv()
+        expert_in(c, 0, n_kv - 1)
+    inv_received()
+    slot_inv = jnp.sum(
+        jnp.where(on_lane, jnp.broadcast_to(inv_in[...], (experts, share, rows)), 0.0),
+        axis=2,
+        keepdims=True,
+    ).reshape(experts * share, 1)
+    inv_wide[...] = jnp.broadcast_to(slot_inv, inv_wide.shape)
+    out_waits[n_kv - 1][0]()
+    for c in range(n_kv):
+        expert_in(c, n_kv - 1, n_kv)
     second_on(wide_items)
     back_waits = []
     for n in range(n_kv):
@@ -412,6 +444,7 @@
         back_waits.append(all_to_all(replies.at[n], returned.at[n], back_sem.at[n]))
     for _, sent in out_waits:
         sent()
+    inv_sent()
     for t in range(items):
         for kind in range(1, 4):
             move(kind, t).wait_send()
@@ -519,6 +552,10 @@
                 pltpu.VMEM((n_kv,) + w_gate.shape[1:], bf16),
                 pltpu.VMEM((n_kv,) + w_up.shape[1:], bf16),
                 pltpu.VMEM((n_kv,) + w_down.shape[1:], bf16),
+                pltpu.VMEM((experts, 1, rows), f32),
+                pltpu.VMEM((experts, 1, rows), f32),
+                pltpu.VMEM((experts * share, w_gate.shape[2]), f32),
+                pltpu.VMEM((n_kv, 2, experts * share, w_gate.shape[2]), f32),
                 pltpu.VMEM((n_kv, experts * share, w_gate.shape[2]), bf16),
                 pltpu.VMEM((n_kv, experts, share, cols), bf16),
                 pltpu.VMEM((n_kv, experts, share, cols), bf16),
@@ -530,6 +567,7 @@
                 dma((2, n_kv - 1)),
                 dma((2, n_kv - 1)),
                 dma((2, 4, 12)),
+                dma((3,)),
                 dma((n_kv, 3)),
                 dma((n_kv, 3)),
                 dma((2, n_kv)),

time: 147 us -> 144 us (0.980)
  Pallas kernels: 144 us -> 142 us
    pallas_call x1, Pallas kernels: 144 us -> 142 us  [per_device(): pl.pallas_call(lambda *refs: layer_kernel(n_ep, n_kv, *refs), name='layer...]
where the time goes in v5:
time: 144 us
  Pallas kernels  142 us (99%)
  local copies, waits for them, and re-layouts  1.57 us (1%)
    pallas_call x1, Pallas kernels, per_device(): pl.pallas_call(lambda *refs: layer_kernel(n_ep, n_kv, *refs), name='layer...  142 us

profile of v5, /device:TPU:24, one launch (start us, length us, event | category | flops | bytes accessed | tf_op | source)
XLA Modules:
  0.0 143.9 jit_solution(16552629817155696857)
XLA Ops:
  0.0 142.4 %layer.1 = bf16[128,512]{1,0:T(8,128)(2,1)} custom-call(bf16[2,2048]{1,0:T(2,128)(2,1)} %refs_0_.1, bf16[768,2048]{1,0:T(8,128)(2,1)} %bitcast.6, bf16[768,2048]{1,0:T(8,128)(2,1)} %bitcast.7, s32[2,1,3]{2,1,0:T(1,128)} %refs_3_.1, s32[2]{0:T(128)} %refs_4_.1, bf16[126,2048]{1,0:T(8,128)(2,1)} %refs_5_.1, bf16[128,512]{1,0:T(8,128)(2,1)} %refs_6_.1, ...), custom_call_target="tpu_custom_call" | custom-call | tf_op jit(solution)/shard_map/layer/pallas_call | solution.py:531
  142.4 1.6 %copy.17 = bf16[128,512]{1,0:T(8,128)(2,1)} copy(bf16[128,512]{1,0:T(8,128)(2,1)} %layer.1) | data formatting | bytes 262144

commit v6 on v5

--- a/solution.py
+++ b/solution.py
@@ -339,20 +339,21 @@
     for copy in scaled_copies:
         copy.wait()
     pump(range(3, 6), range(3, items), range(1, 3))
-    for i in range(1, n_kv - 1):
-        dispatch(i)
+    dispatch(1)
+    pump(range(6, 9), (), range(3, 4))
+    dispatch(2)
+    pump(range(9, items), (), range(4, 6))
     on_lane = iota((experts, share, rows), 2) == iota((experts, share, rows), 1)
     slot_pick = pick_t[...].astype(jnp.float32).reshape(experts, share, rows)
     slot_inv = jnp.sum(slot_pick * inv_t[None], axis=2, keepdims=True)
     inv_out[...] = jnp.sum(jnp.where(on_lane, slot_inv, 0.0), axis=1, keepdims=True)
     inv_received, inv_sent = all_to_all(inv_out, inv_in, inv_sem)
     dispatch(n_kv - 1)
-    second_on(0)
-    for t in range(3, wide_items):
-        pump(range(t + 3, t + 4), (), range(t, t + 1))
-        second_on(t - 2)
-    pump(range(wide_items + 3, items), (), range(wide_items, wide_items + 2))
-    for t in range(wide_items - 2, wide_items):
+    pump((), (), range(6, wide_items))
+    for t in range(4):
+        second_on(t)
+    pump((), (), range(wide_items, wide_items + 2))
+    for t in range(4, wide_items):
         second_on(t)
     pump((), (), range(wide_items + 2, items))
     logits_t = stats[0:experts, :] * inv_t

time: 144 us -> 144 us (level)
  no operation moved by 1% of the time
where the time goes in v6:
time: 144 us
  Pallas kernels  142 us (99%)
  local copies, waits for them, and re-layouts  1.57 us (1%)
    pallas_call x1, Pallas kernels, per_device(): pl.pallas_call(lambda *refs: layer_kernel(n_ep, n_kv, *refs), name='layer...  142 us

profile of v6, /device:TPU:24, one launch (start us, length us, event | category | flops | bytes accessed | tf_op | source)
XLA Modules:
  0.0 143.9 jit_solution(17265743850093212898)
XLA Ops:
  0.0 142.4 %layer.1 = bf16[128,512]{1,0:T(8,128)(2,1)} custom-call(bf16[2,2048]{1,0:T(2,128)(2,1)} %refs_0_.1, bf16[768,2048]{1,0:T(8,128)(2,1)} %bitcast.6, bf16[768,2048]{1,0:T(8,128)(2,1)} %bitcast.7, s32[2,1,3]{2,1,0:T(1,128)} %refs_3_.1, s32[2]{0:T(128)} %refs_4_.1, bf16[126,2048]{1,0:T(8,128)(2,1)} %refs_5_.1, bf16[128,512]{1,0:T(8,128)(2,1)} %refs_6_.1, ...), custom_call_target="tpu_custom_call" | custom-call | tf_op jit(solution)/shard_map/layer/pallas_call | solution.py:532
  142.4 1.6 %copy.17 = bf16[128,512]{1,0:T(8,128)(2,1)} copy(bf16[128,512]{1,0:T(8,128)(2,1)} %layer.1) | data formatting | bytes 262144
